TPU v7x, 32 devices: a whole 2x2x4 slice. The times are simulated.
32 devices in a mesh: grp: 2 (over x), seq: 8 (over z, y), head: 2 (over core).
Axes of the slice: x: 2, y: 2, z: 4, core: 2. Of those that a mesh axis runs over, the one named last changes fastest.
Arguments:
- queries: bfloat16 [16384, 2048], P(('grp', 'seq'), 'head'), parts along dimension 0, may hold values from -6 to 6
- key_states: bfloat16 [16384, 1024], P(('grp', 'seq'), 'head'), parts along dimension 0, may hold values from -6 to 6
- value_states: bfloat16 [16384, 1024], P(('grp', 'seq'), 'head'), parts along dimension 0, may hold values from -6 to 6
- segment_ids: int32 [16384], P(('grp', 'seq')), parts along dimension 0, may hold values from 0 to 15, as said below
Outputs:
- attended: bfloat16 [16384, 2048], P(('grp', 'seq'), 'head'), parts along dimension 0
There are 2 independent parts, one for each index of `grp`. A program takes and returns all parts, laid end to end along the dimension named above; each array names one. Nothing has to cross between parts.
Inputs may be any that keep to these rules, and one draw needn't show every extreme that they name: `segment_ids`: read in logical order, the ids never fall, start at 0 and name all 16 candidates, each one token or more; the first 1536 and the last 1536 logical tokens each lie within one candidate.
All inputs are finite; a program needn't handle non-finite values.
Results may differ from a plain program's by a relative error of at most 0.008.
Values may be sent and summed in bfloat16 or wider, within the bound.
No kernel may reach another device: no remote copies, remote signals or barrier semaphores. Data moves between devices by JAX's collectives and lax.ppermute only.
A program may use at most 64 MiB of HBM per device.

v0:
```python
import functools
import math

import jax
import jax.numpy as jnp
from jax import lax
from jax.experimental import pallas as pl
from jax.experimental.pallas import tpu as pltpu
from jax.sharding import PartitionSpec as P

HEAD_DIM = 128
GROUPS = 2
HALF = 512
PAIR = 2
TILE = 256
TILES = HALF // TILE

EXP_SCALE = 168.0 ** (-0.5) * math.log2(math.e)
HIDDEN = -1e30
MATCH = 12288.0

VMEM = pl.BlockSpec(memory_space=pltpu.VMEM)
SMEM = pl.BlockSpec(memory_space=pltpu.SMEM)
ANY = pl.BlockSpec(memory_space=pl.ANY)
HBM = pl.BlockSpec(memory_space=pltpu.HBM)
PARAMS = pltpu.CompilerParams(vmem_limit_bytes=10 << 20)


def dot_nt(a, b):
    return lax.dot_general(
        a, b, (((1,), (1,)), ((), ())), preferred_element_type=jnp.float32
    )


def dot_nn(a, b):
    return lax.dot_general(
        a, b, (((1,), (0,)), ((), ())), preferred_element_type=jnp.float32
    )


def head_cols(head):
    return slice(head * HEAD_DIM, (head + 1) * HEAD_DIM)


SECOND = HALF + 16
FRONT = SECOND + HALF


def ids_row(ids_v, role):
    row = ids_v[:, role * HALF : (role + 1) * HALF].astype(jnp.float32) + 1.0
    return jnp.broadcast_to(row, (16, HALF)).astype(jnp.bfloat16)


def block_copies(k, v, role, h, target, sem):
    rows = pl.ds(role * HALF, HALF)
    cols = pl.ds(h * PAIR * HEAD_DIM, PAIR * HEAD_DIM)
    return [
        pltpu.make_async_copy(
            src.at[rows, cols],
            target.at[:, pl.ds(part * PAIR * HEAD_DIM, PAIR * HEAD_DIM)],
            sem.at[part],
        )
        for part, src in enumerate((k, v))
    ]


def pack_front_kernel(k, v, ids, f1, front, ids_v, stage, sem, ids_sem, out_sem):
    get_ids = pltpu.make_async_copy(ids, ids_v, ids_sem)
    get_ids.start()
    parts = (pl.ds(0, SECOND), pl.ds(SECOND, HALF))
    copies = [
        block_copies(k, v, 0, h, stage.at[pl.ds(h * SECOND, HALF)], sem.at[h]) for h in range(2)
    ]
    for copy in copies[0] + copies[1]:
        copy.start()
    get_ids.wait()
    stage[HALF:SECOND, :] = ids_row(ids_v, 0)
    first = pl.ds(0, HALF + 8)
    sends = [
        pltpu.make_async_copy(stage.at[first], f1, out_sem.at[0]),
        pltpu.make_async_copy(stage.at[parts[0]], front.at[parts[0]], out_sem.at[1]),
        pltpu.make_async_copy(stage.at[parts[1]], front.at[parts[1]], out_sem.at[2]),
    ]
    for h in range(2):
        for copy in copies[h]:
            copy.wait()
        for send in sends[2 * h : 2 + h]:
            send.start()
    for send in sends:
        send.wait()


def pack_front(k, v, ids):
    return pl.pallas_call(
        pack_front_kernel,
        out_shape=tuple(
            jax.ShapeDtypeStruct((r, HALF), jnp.bfloat16) for r in (HALF + 8, FRONT)
        ),
        in_specs=[HBM] * 3,
        out_specs=[HBM] * 2,
        scratch_shapes=[
            pltpu.VMEM((1, 2 * HALF), jnp.int32),
            pltpu.VMEM((FRONT, HALF), jnp.bfloat16),
            pltpu.SemaphoreType.DMA((2, 2)),
            pltpu.SemaphoreType.DMA,
            pltpu.SemaphoreType.DMA((3,)),
        ],
        compiler_params=PARAMS,
        cost_estimate=pl.CostEstimate(
            flops=1 << 20, bytes_accessed=2 << 20, transcendentals=0
        ),
        name="pack0",
    )(k, v, ids)


def pack_rest_kernel(k, v, ids, b1, f2, b2, ids_v, stage, sem, ids_sem, out_sem):
    get_ids = pltpu.make_async_copy(ids, ids_v, ids_sem)
    get_ids.start()
    pieces = ((1, 0, b1), (0, 1, f2), (1, 1, b2))
    copies = [
        block_copies(k, v, role, h, stage.at[i, pl.ds(0, HALF)], sem.at[i])
        for i, (role, h, _) in enumerate(pieces)
    ]
    for pair in copies:
        for copy in pair:
            copy.start()
    get_ids.wait()
    stage[0, HALF:SECOND, :] = ids_row(ids_v, 1)
    sends = []
    for i, (_, _, piece) in enumerate(pieces):
        for copy in copies[i]:
            copy.wait()
        rows = pl.ds(0, HALF + 8 if i == 0 else HALF)
        sends.append(pltpu.make_async_copy(stage.at[i, rows], piece, out_sem.at[i]))
        sends[-1].start()
    for send in sends:
        send.wait()


def pack_rest(k, v, ids):
    return pl.pallas_call(
        pack_rest_kernel,
        out_shape=tuple(
            jax.ShapeDtypeStruct((r, HALF), jnp.bfloat16) for r in (HALF + 8, HALF, HALF)
        ),
        in_specs=[HBM] * 3,
        out_specs=[HBM] * 3,
        scratch_shapes=[
            pltpu.VMEM((1, 2 * HALF), jnp.int32),
            pltpu.VMEM((3, SECOND, HALF), jnp.bfloat16),
            pltpu.SemaphoreType.DMA((3, 2)),
            pltpu.SemaphoreType.DMA,
            pltpu.SemaphoreType.DMA((3,)),
        ],
        compiler_params=PARAMS,
        cost_estimate=pl.CostEstimate(
            flops=1 << 20, bytes_accessed=3 << 20, transcendentals=0
        ),
        name="pack1",
    )(k, v, ids)


def one_hot_keys(row):
    lane = lax.broadcasted_iota(jnp.int32, (HEAD_DIM, HALF), 0).astype(jnp.float32)
    hot = jnp.where(lane == row.astype(jnp.float32), 1.0, 0.0)
    return hot.T.astype(jnp.bfloat16)


def stacked_queries(q, hot, base, first_head):
    blocks = []
    for i in range(TILES):
        rows = slice(base + i * TILE, base + (i + 1) * TILE)
        mark = hot[rows, :] * jnp.bfloat16(MATCH)
        for j in range(GROUPS):
            blocks.append(jnp.concatenate([q[rows, head_cols(first_head + j)], mark], axis=1))
    return jnp.concatenate(blocks, axis=0)


def with_ones(v):
    return jnp.concatenate([v, jnp.ones(v.shape, v.dtype)], axis=1)


def tile_rows(x, i):
    return x[i * GROUPS * TILE : (i + 1) * GROUPS * TILE]


def edge_mask(above):
    r = lax.broadcasted_iota(jnp.int32, (TILE, TILE), 0)
    c = lax.broadcasted_iota(jnp.int32, (TILE, TILE), 1)
    return jnp.concatenate([c > r if above else c <= r] * GROUPS, axis=0)


def triangle_scores(q2, k_aug, above):
    mask = edge_mask(above)
    seen = [[] for _ in range(TILES)]
    for t in range(TILES):
        first, end = (0, t + 1) if above else (t, TILES)
        rows = q2[first * GROUPS * TILE : end * GROUPS * TILE]
        s = dot_nt(rows, k_aug[t * TILE : (t + 1) * TILE])
        for i in range(first, end):
            part = tile_rows(s, i - first)
            if i == t:
                part = jnp.where(mask, part, HIDDEN)
            seen[i].append(part)
    return seen


def triangle_values(probs, v_aug, above):
    total = [None] * TILES
    for t in range(TILES):
        first, end = (0, t + 1) if above else (t, TILES)
        rows = jnp.concatenate(
            [probs[i][t - i if above else t] for i in range(first, end)], axis=0
        )
        o = dot_nn(rows, v_aug[t * TILE : (t + 1) * TILE])
        for i in range(first, end):
            part = tile_rows(o, i - first)
            total[i] = part if total[i] is None else total[i] + part
    return total


def row_max(parts):
    top = parts[0]
    for part in parts[1:]:
        top = jnp.maximum(top, part)
    return jnp.max(top, axis=-1, keepdims=True)


def weights(parts, m):
    wide = jnp.concatenate([m] * (TILE // HEAD_DIM), axis=1)
    return [jnp.exp2((part - wide) * EXP_SCALE).astype(jnp.bfloat16) for part in parts]


def state_slices(base, g):
    for i in range(TILES):
        for j in range(GROUPS):
            rows = slice(base + i * TILE, base + (i + 1) * TILE)
            yield i, slice(j * TILE, (j + 1) * TILE), rows, head_cols(GROUPS * g + j)


def load_state(ref, base, g):
    parts = [[] for _ in range(TILES)]
    for i, _, rows, cols in state_slices(base, g):
        parts[i].append(ref[rows, cols])
    return [jnp.concatenate(p, axis=0) for p in parts]


def own_kernel(h, q, k, v, hot, acc, mx, ls):
    for role in range(2):
        base = role * HALF
        seen = slice(base, base + HALF)
        for g in range(PAIR):
            own = head_cols(PAIR * h + g)
            q2 = stacked_queries(q, hot, base, (PAIR * h + g) * GROUPS)
            k_aug = jnp.concatenate([k[seen, own], hot[seen, :]], axis=1)
            scores = triangle_scores(q2, k_aug, False)
            tops = [
                jnp.broadcast_to(row_max(parts), (GROUPS * TILE, HEAD_DIM)) for parts in scores
            ]
            probs = [weights(parts, m) for parts, m in zip(scores, tops)]
            o = triangle_values(probs, with_ones(v[seen, own]), False)
            for i, mine, rows, cols in state_slices(base, g):
                acc[rows, cols] = o[i][mine, :HEAD_DIM]
                ls[rows, cols] = o[i][mine, HEAD_DIM:]
                mx[rows, cols] = tops[i][mine]


STATE = jax.ShapeDtypeStruct((2 * HALF, 2 * PAIR * HEAD_DIM), jnp.float32)


def cost(gflop):
    return pl.CostEstimate(
        flops=gflop << 30, bytes_accessed=8 << 20, transcendentals=2 << 20
    )


def own(h, q, k, v, hot):
    return pl.pallas_call(
        functools.partial(own_kernel, h),
        out_shape=(STATE,) * 3,
        in_specs=[VMEM] * 4,
        out_specs=[VMEM] * 3,
        compiler_params=PARAMS,
        cost_estimate=cost(5),
    )(q, k, v, hot)


def far_kernel(h, n, idx, q, hot, zp, za, zb, pa, pb, *rest):
    (acc0, mx0, ls0), (acc, mx, ls) = rest[:3], rest[3:6]
    far, seg, sem, seg_sem = rest[6:]
    from_partner = idx[0] >= n - 2
    id_rows = pl.ds(HALF, 8)

    def fetch(role, src):
        return pltpu.make_async_copy(src, far.at[role], sem.at[role])

    def fetch_ids(role, src):
        return pltpu.make_async_copy(src, seg.at[role], seg_sem.at[role])

    pair = pl.ds(h * SECOND, HALF)
    whole = pl.ds(0, HALF)
    back = (za.at[whole], zb)[h]
    partner = (pa.at[whole], pb)[h]
    fetch_ids(0, zp.at[id_rows]).start()
    fetch(0, zp.at[pair]).start()

    @pl.when(from_partner)
    def _():
        fetch_ids(1, pa.at[id_rows]).start()
        fetch(1, partner).start()

    @pl.when(jnp.logical_not(from_partner))
    def _():
        fetch_ids(1, za.at[id_rows]).start()
        fetch(1, back).start()

    for role in range(2):
        fetch_ids(role, zp.at[id_rows]).wait()
    hots = [one_hot_keys(seg[role, 0:1, :]) for role in range(2)]
    for role in range(2):
        fetch(role, zp.at[pair]).wait()
    for role in range(2):
        base = role * HALF
        for g in range(PAIR):
            q2 = stacked_queries(q, hot, base, (PAIR * h + g) * GROUPS)
            keys = far[role, :, head_cols(g)]
            k_aug = jnp.concatenate([keys, hots[role]], axis=1)
            scores = triangle_scores(q2, k_aug, True)
            old = load_state(mx0, base, g)
            tops = [jnp.maximum(m, row_max(parts)) for m, parts in zip(old, scores)]
            probs = [weights(parts, m) for parts, m in zip(scores, tops)]
            v_aug = with_ones(far[role, :, head_cols(PAIR + g)])
            o = triangle_values(probs, v_aug, True)
            for i, mine, rows, cols in state_slices(base, g):
                keep = jnp.exp2((old[i][mine] - tops[i][mine]) * EXP_SCALE)
                acc[rows, cols] = keep * acc0[rows, cols] + o[i][mine, :HEAD_DIM]
                ls[rows, cols] = keep * ls0[rows, cols] + o[i][mine, HEAD_DIM:]
                mx[rows, cols] = tops[i][mine]


def far(h, n, idx, q, hot, zp, za, zb, pa, pb, state):
    return pl.pallas_call(
        functools.partial(far_kernel, h, n),
        out_shape=(STATE,) * 3,
        in_specs=[SMEM] + [VMEM] * 2 + [ANY] * 5 + [VMEM] * 3,
        out_specs=[VMEM] * 3,
        scratch_shapes=[
            pltpu.VMEM((2, HALF, HALF), jnp.bfloat16),
            pltpu.VMEM((2, 8, HALF), jnp.bfloat16),
            pltpu.SemaphoreType.DMA((2,)),
            pltpu.SemaphoreType.DMA((2,)),
        ],
        compiler_params=PARAMS,
        cost_estimate=cost(5),
    )(idx, q, hot, zp, za, zb, pa, pb, *state)


def finish(h, role, q, hot, piece, hot_mid, state, out, o_buf, out_sem):
    acc, mx, ls = state
    base = role * HALF
    sends = []
    for g in range(PAIR):
        q2 = stacked_queries(q, hot, base, (PAIR * h + g) * GROUPS)
        k_aug = jnp.concatenate([piece[0:HALF, head_cols(g)], hot_mid], axis=1)
        v_aug = with_ones(piece[0:HALF, head_cols(PAIR + g)])
        for t in range(TILES):
            s = dot_nt(tile_rows(q2, t), k_aug)
            old = load_state(mx, base, g)[t]
            m = jnp.maximum(old, jnp.max(s, axis=-1, keepdims=True))
            keep = jnp.exp2((old - m) * EXP_SCALE)
            wide = jnp.concatenate([m] * (HALF // HEAD_DIM), axis=1)
            p = jnp.exp2((s - wide) * EXP_SCALE).astype(jnp.bfloat16)
            o = dot_nn(p, v_aug)
            for i, mine, rows, cols in state_slices(base, g):
                if i != t:
                    continue
                total = keep[mine] * ls[rows, cols] + o[mine, HEAD_DIM:]
                value = keep[mine] * acc[rows, cols] + o[mine, :HEAD_DIM]
                o_buf[rows, cols] = (value * (1.0 / total)).astype(jnp.bfloat16)
        part = pl.ds(g * GROUPS * HEAD_DIM, GROUPS * HEAD_DIM)
        to = pl.ds((PAIR * h + g) * GROUPS * HEAD_DIM, GROUPS * HEAD_DIM)
        here = pl.ds(base, HALF)
        sends.append(
            pltpu.make_async_copy(
                o_buf.at[here, part], out.at[here, to], out_sem.at[PAIR * role + g]
            )
        )
        sends[-1].start()
    return sends


def first_pair_kernel(
    n, idx, q, hot, r1, pa, pb, d1, f1, k, v, *rest
):
    state1, state2 = rest[:3], rest[3:6]
    out, hots, mid, seg, sem, extra, extra_sem, o_buf, out_sem = rest[6:]
    odd = idx[0] % 2 == 1
    end = idx[0] == n - 1
    width = PAIR * HEAD_DIM
    whole, id_rows = pl.ds(0, HALF), pl.ds(HALF, 8)
    cols = [pl.ds(part * width, width) for part in range(2)]

    def fetch(role, ids, srcs):
        pltpu.make_async_copy(ids.at[id_rows], seg.at[role], sem.at[role, 2]).start()
        for i, src in enumerate(srcs):
            pltpu.make_async_copy(src, mid.at[role, :, cols[i]], sem.at[role, i]).start()

    def columns(ref):
        return [ref.at[whole, c] for c in cols]

    def own_front(h):
        return [x.at[whole, pl.ds(h * width, width)] for x in (k, v)]

    def fetch_extra(role, srcs):
        return [
            pltpu.make_async_copy(src, extra.at[role, :, cols[i]], extra_sem.at[role, i])
            for i, src in enumerate(srcs)
        ]

    for role, local, here, sent in ((0, odd, pa, r1), (1, end, None, d1)):

        @pl.when(local)
        def _():
            if role == 0:
                fetch(role, here, columns(here))
                srcs = columns(pb)
            else:
                fetch(role, f1, own_front(0))
                srcs = own_front(1)
            for copy in fetch_extra(role, srcs):
                copy.start()

        @pl.when(jnp.logical_not(local))
        def _():
            fetch(role, sent, columns(sent))

    for role in range(2):
        for i in range(2):
            pltpu.make_async_copy(
                pa.at[whole, cols[i]], mid.at[role, :, cols[i]], sem.at[role, i]
            ).wait()
        pltpu.make_async_copy(pa.at[id_rows], seg.at[role], sem.at[role, 2]).wait()
    sends = []
    for role in range(2):
        hot_mid = one_hot_keys(seg[role, 0:1, :])
        hots[role] = hot_mid
        sends += finish(
            0, role, q, hot, mid.at[role], hot_mid, state1, out, o_buf, out_sem
        )
    for copy in sends:
        copy.wait()

    @pl.when(idx[0] == 0)
    def _():
        acc, _, ls = state2
        o_buf[0:HALF, :] = (acc[0:HALF, :] * (1.0 / ls[0:HALF, :])).astype(jnp.bfloat16)
        second = pl.ds(2 * width, 2 * width)
        copy = pltpu.make_async_copy(
            o_buf.at[whole], out.at[whole, second], out_sem.at[0]
        )
        copy.start()
        copy.wait()

    for role, local in ((0, odd), (1, end)):

        @pl.when(local)
        def _():
            for copy in fetch_extra(role, columns(pb)):
                copy.wait()
            for copy in finish(
                1, role, q, hot, extra.at[role], hots[role], state2, out, o_buf, out_sem
            ):
                copy.wait()


OUT_SCRATCH = (
    pltpu.VMEM((2 * HALF, 2 * PAIR * HEAD_DIM), jnp.bfloat16),
    pltpu.SemaphoreType.DMA((2 * PAIR,)),
)


def first_pair(n, idx, q, hot, pieces, state1, state2):
    piece = pltpu.VMEM((2, HALF, HALF), jnp.bfloat16)
    return pl.pallas_call(
        functools.partial(first_pair_kernel, n),
        out_shape=(
            jax.ShapeDtypeStruct(q.shape, q.dtype),
            jax.ShapeDtypeStruct((2, HALF, HEAD_DIM), jnp.bfloat16),
        ),
        in_specs=[SMEM] + [VMEM] * 2 + [ANY] * len(pieces) + [VMEM] * 6,
        out_specs=(ANY, VMEM),
        scratch_shapes=[
            piece,
            pltpu.VMEM((2, 8, HALF), jnp.bfloat16),
            pltpu.SemaphoreType.DMA((2, 3)),
            piece,
            pltpu.SemaphoreType.DMA((2, 2)),
            *OUT_SCRATCH,
        ],
        compiler_params=PARAMS,
        cost_estimate=cost(5),
        name="last0",
    )(idx, q, hot, *pieces, *state1, *state2)


def second_pair_kernel(role, n, idx, q, hot, piece, hots, acc, mx, ls, _, out, o_buf, out_sem):
    if role == 0:
        needed = (idx[0] % 2 == 0) & (idx[0] > 0)
    else:
        needed = idx[0] < n - 1

    @pl.when(needed)
    def _():
        state = (acc, mx, ls)
        for copy in finish(
            1, role, q, hot, piece, hots[role], state, out, o_buf, out_sem
        ):
            copy.wait()


def second_pair(role, n, idx, q, hot, piece, hots, state, out):
    return pl.pallas_call(
        functools.partial(second_pair_kernel, role, n),
        out_shape=jax.ShapeDtypeStruct(q.shape, q.dtype),
        in_specs=[SMEM] + [VMEM] * 7 + [ANY],
        out_specs=ANY,
        input_output_aliases={8: 0},
        scratch_shapes=OUT_SCRATCH,
        compiler_params=PARAMS,
        cost_estimate=cost(5),
    )(idx, q, hot, piece, hots, *state, out)


def body(queries, key_states, value_states, segment_ids):
    n = lax.axis_size("seq")
    seq = lax.axis_index("seq").astype(jnp.int32)
    idx = seq.reshape(1)
    lane = jnp.arange(HEAD_DIM, dtype=jnp.int32)
    hot = (segment_ids[:, None] + 1 == lane[None, :]).astype(jnp.bfloat16)

    partner = [(i, i ^ 1) for i in range(n)]
    up_two = [(i, i + 2) for i in range(n - 2)]
    down_two = [(i + 2, i) for i in range(n - 2)]
    relay = [(i, i + 2) for i in range(0, n - 2, 2)]

    def send(x, route):
        return lax.ppermute(x, "seq", route)

    q, k, v = queries, key_states, value_states
    in_hbm = tuple(
        pltpu.with_memory_space_constraint(x, pltpu.HBM)
        for x in (k, v, segment_ids.reshape(1, 2 * HALF))
    )
    f1, front = pack_front(*in_hbm)
    pa = send(f1, partner)
    zp = send(front, up_two)
    b1, f2, b2 = pack_rest(*in_hbm)
    za = send(b1, down_two)
    pb = send(f2, partner)
    zb = send(b2, down_two)
    state1 = own(0, q, k, v, hot)
    r1 = send(pa, relay)
    state2 = own(1, q, k, v, hot)
    even = seq % 2 == 0
    back = jnp.where(even, za, b1)
    d1 = send(back, partner)
    r2 = send(pb, relay)
    state1 = far(0, n, idx, q, hot, zp, za, za, pa, pa, state1)
    back = jnp.where(even, zb, b2)
    d2 = send(back, partner)
    state2 = far(1, n, idx, q, hot, zp, za, zb, pa, pb, state2)

    pieces = (r1, pa, pb, d1, f1, k, v)
    out, hots = first_pair(n, idx, q, hot, pieces, state1, state2)
    out = second_pair(1, n, idx, q, hot, d2, hots, state2, out)
    return second_pair(0, n, idx, q, hot, r2, hots, state2, out)


def solution(mesh):
    in_specs = (
        P(("grp", "seq"), "head"),
        P(("grp", "seq"), "head"),
        P(("grp", "seq"), "head"),
        P(("grp", "seq")),
    )
    out_specs = P(("grp", "seq"), "head")
    return jax.shard_map(body, mesh=mesh, in_specs=in_specs, out_specs=out_specs, check_vma=False)
```

profile of v0, /device:TPU:24, one launch (start us, length us, event | category | flops | bytes accessed | tf_op | source)
XLA Modules:
  0.0 71.7 jit_solution(9976247349261476110)
XLA Ops:
  0.0 2.4 %pack1.1 = (bf16[520,512]{1,0:T(8,128)(2,1)S(1)}, bf16[512,512]{1,0:T(8,128)(2,1)}, bf16[512,512]{1,0:T(8,128)(2,1)}) custom-call(bf16[1024,512]{1,0:T(8,128)(2,1)} %k.9, bf16[1024,512]{1,0:T(8,128)(2,1)} %v.9, s32[1,1024]{1,0:T(1,128)} %bitcast.2), custom_call_target="tpu_custom_call" | custom-call | flops 1048576 | bytes 3145728 | tf_op jit(solution)/shard_map/pack1/pallas_call | solution.py:141
  2.4 2.4 %collective-permute-start.4 = (bf16[520,512]{1,0:T(8,128)(2,1)S(1)}, bf16[520,512]{1,0:T(8,128)(2,1)S(1)}, u32[]{:S(2)}, u32[]{:S(2)}) collective-permute-start(bf16[520,512]{1,0:T(8,128)(2,1)S(1)} %get-tuple-element.26), channel_id=1, source_target_pairs={{4,0},{6,2},{8,4},{10,6},{12,8},{14,10},{5,1},{7,3},{9,5},{11,7},{... | collective-permute-start | bytes 1597448 | tf_op jit(solution)/shard_map/ppermute | solution.py:547
  4.8 2.4 %pack0.1 = (bf16[520,512]{1,0:T(8,128)(2,1)}, bf16[1040,512]{1,0:T(8,128)(2,1)}) custom-call(bf16[1024,512]{1,0:T(8,128)(2,1)} %k.9, bf16[1024,512]{1,0:T(8,128)(2,1)} %v.9, s32[1,1024]{1,0:T(1,128)} %bitcast.3), custom_call_target="tpu_custom_call" | custom-call | flops 1048576 | bytes 2097152 | tf_op jit(solution)/shard_map/pack0/pallas_call | solution.py:94
  7.2 1.6 %collective-permute-start.2 = (bf16[520,512]{1,0:T(8,128)(2,1)}, bf16[520,512]{1,0:T(8,128)(2,1)}, u32[]{:S(2)}, u32[]{:S(2)}) collective-permute-start(bf16[520,512]{1,0:T(8,128)(2,1)} %get-tuple-element.25.f1), channel_id=1, source_target_pairs={{0,2},{2,0},{4,6},{6,4},{8,10},{10,8},{12,14},{14,12},{1,3},{3,1},... | collective-permute-start | bytes 1597448 | tf_op jit(solution)/shard_map/ppermute | solution.py:547
  9.3 3.1 %collective-permute-start.7 = (bf16[512,512]{1,0:T(8,128)(2,1)}, bf16[512,512]{1,0:T(8,128)(2,1)}, u32[]{:S(2)}, u32[]{:S(2)}) collective-permute-start(bf16[512,512]{1,0:T(8,128)(2,1)} %get-tuple-element.34), channel_id=1, source_target_pairs={{4,0},{6,2},{8,4},{10,6},{12,8},{14,10},{5,1},{7,3},{9,5},{11,7},{... | collective-permute-start | bytes 1572872 | tf_op jit(solution)/shard_map/ppermute | solution.py:547
  12.4 1.3 %collective-permute-start.6 = (bf16[1040,512]{1,0:T(8,128)(2,1)}, bf16[1040,512]{1,0:T(8,128)(2,1)}, u32[]{:S(2)}, u32[]{:S(2)}) collective-permute-start(bf16[1040,512]{1,0:T(8,128)(2,1)} %get-tuple-element.27), channel_id=1, source_target_pairs={{0,4},{2,6},{4,8},{6,10},{8,12},{10,14},{1,5},{3,7},{5,9},{7,11},{... | collective-permute-start | bytes 3194888 | tf_op jit(solution)/shard_map/ppermute | solution.py:547
  14.0 2.2 %shard_map.48 = (f32[1024,512]{1,0:T(8,128)S(1)}, f32[1024,512]{1,0:T(8,128)S(1)}, f32[1024,512]{1,0:T(8,128)S(1)}) custom-call(bf16[1024,1024]{1,0:T(8,128)(2,1)S(1)} %copy-done.2, bf16[1024,512]{1,0:T(8,128)(2,1)S(1)} %copy-done, bf16[1024,512]{1,0:T(8,128)(2,1)S(1)} %copy-done.1, bf16[1024,128]{1,0:T(8,128)(2,1)S(1)} %fusion.hot), custom_call_target="tpu_custom_call" | custom-call | flops 5368709120 | bytes 8388608 | tf_op jit(solution)/shard_map/pallas_call | solution.py:278
  16.2 1.4 %copy-done.10 = f32[1024,512]{1,0:T(8,128)} copy-done((f32[1024,512]{1,0:T(8,128)}, f32[1024,512]{1,0:T(8,128)S(1)}, u32[]{:S(2)}) %copy-start.10) | copy-done | bytes 2097176
  17.6 1.4 %copy-done.12 = f32[1024,512]{1,0:T(8,128)} copy-done((f32[1024,512]{1,0:T(8,128)}, f32[1024,512]{1,0:T(8,128)S(1)}, u32[]{:S(2)}) %copy-start.12) | copy-done | bytes 2097176
  19.0 1.4 %copy-done.14 = f32[1024,512]{1,0:T(8,128)} copy-done((f32[1024,512]{1,0:T(8,128)}, f32[1024,512]{1,0:T(8,128)S(1)}, u32[]{:S(2)}) %copy-start.14) | copy-done | bytes 2097176
  20.3 2.2 %shard_map.46 = (f32[1024,512]{1,0:T(8,128)S(1)}, f32[1024,512]{1,0:T(8,128)S(1)}, f32[1024,512]{1,0:T(8,128)S(1)}) custom-call(bf16[1024,1024]{1,0:T(8,128)(2,1)S(1)} %copy-done.2, bf16[1024,512]{1,0:T(8,128)(2,1)S(1)} %copy-done, bf16[1024,512]{1,0:T(8,128)(2,1)S(1)} %copy-done.1, bf16[1024,128]{1,0:T(8,128)(2,1)S(1)} %fusion.hot), custom_call_target="tpu_custom_call" | custom-call | flops 5368709120 | bytes 8388608 | tf_op jit(solution)/shard_map/pallas_call | solution.py:278
  22.6 1.3 %copy-done.4 = f32[1024,512]{1,0:T(8,128)} copy-done((f32[1024,512]{1,0:T(8,128)}, f32[1024,512]{1,0:T(8,128)S(1)}, u32[]{:S(2)}) %copy-start.4) | copy-done | bytes 2097176
  23.9 1.4 %copy-done.6 = f32[1024,512]{1,0:T(8,128)} copy-done((f32[1024,512]{1,0:T(8,128)}, f32[1024,512]{1,0:T(8,128)S(1)}, u32[]{:S(2)}) %copy-start.6) | copy-done | bytes 2097176
  25.3 1.3 %copy-done.8 = f32[1024,512]{1,0:T(8,128)} copy-done((f32[1024,512]{1,0:T(8,128)}, f32[1024,512]{1,0:T(8,128)S(1)}, u32[]{:S(2)}) %copy-start.8) | copy-done | bytes 2097176
  26.6 0.9 %collective-permute-done.7.zb = bf16[512,512]{1,0:T(8,128)(2,1)} collective-permute-done((bf16[512,512]{1,0:T(8,128)(2,1)}, bf16[512,512]{1,0:T(8,128)(2,1)}, u32[]{:S(2)}, u32[]{:S(2)}) %collective-permute-start.7) | collective-permute-done | bytes 524320 | tf_op jit(solution)/shard_map/ppermute | solution.py:547
  27.5 1.1 %broadcast_select_fusion.1 = bf16[512,512]{1,0:T(8,128)(2,1)S(1)} fusion(bf16[512,512]{1,0:T(8,128)(2,1)} %collective-permute-done.7.zb, bf16[512,512]{1,0:T(8,128)(2,1)} %get-tuple-element.34, pred[]{:T(512)S(6)} %eq.21), kind=kLoop, calls=%fused_computation.3 | loop fusion | flops 262144 | bytes 1572865 | tf_op jit(solution)/shard_map/jit(_where)/select_n | solution.py:569
  28.6 1.6 %collective-permute-start.8 = (bf16[512,512]{1,0:T(8,128)(2,1)S(1)}, bf16[512,512]{1,0:T(8,128)(2,1)S(1)}, u32[]{:S(2)}, u32[]{:S(2)}) collective-permute-start(bf16[512,512]{1,0:T(8,128)(2,1)S(1)} %broadcast_select_fusion.1), channel_id=1, source_target_pairs={{0,2},{2,0},{4,6},{6,4},{8,10},{10,8},{12,14},{14,12},{1,3},{3,1},... | collective-permute-start | bytes 1572872 | tf_op jit(solution)/shard_map/ppermute | solution.py:547
  30.2 3.6 %collective-permute-done.pb = bf16[512,512]{1,0:T(8,128)(2,1)} collective-permute-done((bf16[512,512]{1,0:T(8,128)(2,1)}, bf16[512,512]{1,0:T(8,128)(2,1)}, u32[]{:S(2)}, u32[]{:S(2)}) %collective-permute-start) | collective-permute-done | bytes 524320 | tf_op jit(solution)/shard_map/ppermute | solution.py:547
  33.8 1.3 %collective-permute-start.1 = (bf16[512,512]{1,0:T(8,128)(2,1)}, bf16[512,512]{1,0:T(8,128)(2,1)S(1)}, u32[]{:S(2)}, u32[]{:S(2)}) collective-permute-start(bf16[512,512]{1,0:T(8,128)(2,1)} %collective-permute-done.pb), channel_id=1, source_target_pairs={{0,4},{4,8},{8,12},{1,5},{5,9},{9,13},{16,20},{20,24},{24,28},{17,... | collective-permute-start | bytes 1572872 | tf_op jit(solution)/shard_map/ppermute | solution.py:547
  35.2 1.0 %collective-permute-start.5 = (bf16[520,512]{1,0:T(8,128)(2,1)S(1)}, bf16[520,512]{1,0:T(8,128)(2,1)S(1)}, u32[]{:S(2)}, u32[]{:S(2)}) collective-permute-start(bf16[520,512]{1,0:T(8,128)(2,1)S(1)} %broadcast_select_fusion), channel_id=1, source_target_pairs={{0,2},{2,0},{4,6},{6,4},{8,10},{10,8},{12,14},{14,12},{1,3},{3,1},... | collective-permute-start | bytes 1597448 | tf_op jit(solution)/shard_map/ppermute | solution.py:547
  36.2 1.3 %collective-permute-start.3 = (bf16[520,512]{1,0:T(8,128)(2,1)}, bf16[520,512]{1,0:T(8,128)(2,1)S(1)}, u32[]{:S(2)}, u32[]{:S(2)}) collective-permute-start(bf16[520,512]{1,0:T(8,128)(2,1)} %collective-permute-done.2.pa.pb), channel_id=1, source_target_pairs={{0,4},{4,8},{8,12},{1,5},{5,9},{9,13},{16,20},{20,24},{24,28},{17,... | collective-permute-start | bytes 1597448 | tf_op jit(solution)/shard_map/ppermute | solution.py:547
  37.4 3.6 %collective-permute-done.6.zp = bf16[1040,512]{1,0:T(8,128)(2,1)} collective-permute-done((bf16[1040,512]{1,0:T(8,128)(2,1)}, bf16[1040,512]{1,0:T(8,128)(2,1)}, u32[]{:S(2)}, u32[]{:S(2)}) %collective-permute-start.6) | collective-permute-done | bytes 1064992 | tf_op jit(solution)/shard_map/ppermute | solution.py:547
  41.0 1.6 %copy-done.11 = f32[1024,512]{1,0:T(8,128)S(1)} copy-done((f32[1024,512]{1,0:T(8,128)S(1)}, f32[1024,512]{1,0:T(8,128)}, u32[]{:S(2)}) %copy-start.11) | copy-done | bytes 2097176
  42.6 1.6 %copy-done.13 = f32[1024,512]{1,0:T(8,128)S(1)} copy-done((f32[1024,512]{1,0:T(8,128)S(1)}, f32[1024,512]{1,0:T(8,128)}, u32[]{:S(2)}) %copy-start.13) | copy-done | bytes 2097176
  44.2 1.6 %copy-done.15 = f32[1024,512]{1,0:T(8,128)S(1)} copy-done((f32[1024,512]{1,0:T(8,128)S(1)}, f32[1024,512]{1,0:T(8,128)}, u32[]{:S(2)}) %copy-start.15) | copy-done | bytes 2097176
  45.8 4.1 %shard_map.49 = (f32[1024,512]{1,0:T(8,128)S(1)}, f32[1024,512]{1,0:T(8,128)S(1)}, f32[1024,512]{1,0:T(8,128)S(1)}) custom-call(s32[1]{0:T(128)} %bitcast.idx, bf16[1024,1024]{1,0:T(8,128)(2,1)S(1)} %copy-done.3, bf16[1024,128]{1,0:T(8,128)(2,1)S(1)} %fusion.hot, bf16[1040,512]{1,0:T(8,128)(2,1)} %collective-permute-done.6.zp, ...), custom_call_target="tpu_custom_call" | custom-call | flops 5368709120 | bytes 8388608 | tf_op jit(solution)/shard_map/pallas_call | solution.py:342
  49.9 4.0 %shard_map.47 = (f32[1024,512]{1,0:T(8,128)S(1)}, f32[1024,512]{1,0:T(8,128)S(1)}, f32[1024,512]{1,0:T(8,128)S(1)}) custom-call(s32[1]{0:T(128)} %bitcast.idx, bf16[1024,1024]{1,0:T(8,128)(2,1)S(1)} %copy-done.3, bf16[1024,128]{1,0:T(8,128)(2,1)S(1)} %fusion.hot, bf16[1040,512]{1,0:T(8,128)(2,1)} %collective-permute-done.6.zp, ...), custom_call_target="tpu_custom_call" | custom-call | flops 5368709120 | bytes 8388608 | tf_op jit(solution)/shard_map/pallas_call | solution.py:342
  53.9 1.0 %collective-permute-done.5.d1 = bf16[520,512]{1,0:T(8,128)(2,1)S(1)} collective-permute-done((bf16[520,512]{1,0:T(8,128)(2,1)S(1)}, bf16[520,512]{1,0:T(8,128)(2,1)S(1)}, u32[]{:S(2)}, u32[]{:S(2)}) %collective-permute-start.5) | collective-permute-done | bytes 532512 | tf_op jit(solution)/shard_map/ppermute | solution.py:547
  54.9 6.4 %collective-permute-done.3.r1 = bf16[520,512]{1,0:T(8,128)(2,1)S(1)} collective-permute-done((bf16[520,512]{1,0:T(8,128)(2,1)}, bf16[520,512]{1,0:T(8,128)(2,1)S(1)}, u32[]{:S(2)}, u32[]{:S(2)}) %collective-permute-start.3) | collective-permute-done | bytes 532512 | tf_op jit(solution)/shard_map/ppermute | solution.py:547
  61.3 4.8 %last0.1 = (bf16[1024,1024]{1,0:T(8,128)(2,1)}, bf16[2,512,128]{2,1,0:T(8,128)(2,1)S(1)}) custom-call(s32[1]{0:T(128)} %bitcast.idx, bf16[1024,1024]{1,0:T(8,128)(2,1)S(1)} %copy-done.3, bf16[1024,128]{1,0:T(8,128)(2,1)S(1)} %fusion.hot, bf16[520,512]{1,0:T(8,128)(2,1)S(1)} %collective-permute-done.3.r1, bf16[520,512]{1,0:T(8,128)(2,1)} %collective-permute-done.2.pa.pb, ...), custom_call_target="tpu_custom_call" | custom-call | flops 5368709120 | bytes 8388608 | tf_op jit(solution)/shard_map/last0/pallas_call | solution.py:484
  66.1 2.7 %shard_map.50._ = bf16[1024,1024]{1,0:T(8,128)(2,1)} custom-call(s32[1]{0:T(128)} %bitcast.idx, bf16[1024,1024]{1,0:T(8,128)(2,1)S(1)} %copy-done.3, bf16[1024,128]{1,0:T(8,128)(2,1)S(1)} %fusion.hot, bf16[512,512]{1,0:T(8,128)(2,1)S(1)} %collective-permute-done.8.piece, ...), custom_call_target="tpu_custom_call", output_to_operand_aliasing={{}: (8, {})} | custom-call | flops 5368709120 | bytes 8388608 | tf_op jit(solution)/shard_map/pallas_call | solution.py:522
  68.8 2.7 %shard_map.51 = bf16[1024,1024]{1,0:T(8,128)(2,1)} custom-call(s32[1]{0:T(128)} %bitcast.idx, bf16[1024,1024]{1,0:T(8,128)(2,1)S(1)} %copy-done.3, bf16[1024,128]{1,0:T(8,128)(2,1)S(1)} %fusion.hot, bf16[512,512]{1,0:T(8,128)(2,1)S(1)} %collective-permute-done.1.piece, ...), custom_call_target="tpu_custom_call", output_to_operand_aliasing={{}: (8, {})} | custom-call | flops 5368709120 | bytes 8388608 | tf_op jit(solution)/shard_map/pallas_call | solution.py:522
  (33 shorter events, 0.8 us)
Async XLA Ops:
  0.0 13.7 %copy-start.16 = (s32[1024]{0:T(1024)S(1)}, s32[1024]{0:T(1024)}, u32[]{:S(2)}) copy-start(s32[1024]{0:T(1024)} %param.7) | copy-start | bytes 12292
  0.0 13.9 %copy-start = (bf16[1024,512]{1,0:T(8,128)(2,1)S(1)}, bf16[1024,512]{1,0:T(8,128)(2,1)}, u32[]{:S(2)}) copy-start(bf16[1024,512]{1,0:T(8,128)(2,1)} %k.9) | copy-start | bytes 3145732
  0.0 13.9 %copy-start.1 = (bf16[1024,512]{1,0:T(8,128)(2,1)S(1)}, bf16[1024,512]{1,0:T(8,128)(2,1)}, u32[]{:S(2)}) copy-start(bf16[1024,512]{1,0:T(8,128)(2,1)} %v.9) | copy-start | bytes 3145732
  0.0 14.0 %copy-start.2 = (bf16[1024,1024]{1,0:T(8,128)(2,1)S(1)}, bf16[1024,1024]{1,0:T(8,128)(2,1)}, u32[]{:S(2)}) copy-start(bf16[1024,1024]{1,0:T(8,128)(2,1)} %q.13) | copy-start | bytes 6291460
  2.4 32.6 %collective-permute-start.4 = (bf16[520,512]{1,0:T(8,128)(2,1)S(1)}, bf16[520,512]{1,0:T(8,128)(2,1)S(1)}, u32[]{:S(2)}, u32[]{:S(2)}) collective-permute-start(bf16[520,512]{1,0:T(8,128)(2,1)S(1)} %get-tuple-element.26), channel_id=1, source_target_pairs={{4,0},{6,2},{8,4},{10,6},{12,8},{14,10},{5,1},{7,3},{9,5},{11,7},{... | collective-permute-start | bytes 1597448 | tf_op jit(solution)/shard_map/ppermute | solution.py:547
  7.2 28.9 %collective-permute-start.2 = (bf16[520,512]{1,0:T(8,128)(2,1)}, bf16[520,512]{1,0:T(8,128)(2,1)}, u32[]{:S(2)}, u32[]{:S(2)}) collective-permute-start(bf16[520,512]{1,0:T(8,128)(2,1)} %get-tuple-element.25.f1), channel_id=1, source_target_pairs={{0,2},{2,0},{4,6},{6,4},{8,10},{10,8},{12,14},{14,12},{1,3},{3,1},... | collective-permute-start | bytes 1597448 | tf_op jit(solution)/shard_map/ppermute | solution.py:547
  8.8 25.0 %collective-permute-start = (bf16[512,512]{1,0:T(8,128)(2,1)}, bf16[512,512]{1,0:T(8,128)(2,1)}, u32[]{:S(2)}, u32[]{:S(2)}) collective-permute-start(bf16[512,512]{1,0:T(8,128)(2,1)} %get-tuple-element.24), channel_id=1, source_target_pairs={{0,2},{2,0},{4,6},{6,4},{8,10},{10,8},{12,14},{14,12},{1,3},{3,1},... | collective-permute-start | bytes 1572872 | tf_op jit(solution)/shard_map/ppermute | solution.py:547
  9.3 18.2 %collective-permute-start.7 = (bf16[512,512]{1,0:T(8,128)(2,1)}, bf16[512,512]{1,0:T(8,128)(2,1)}, u32[]{:S(2)}, u32[]{:S(2)}) collective-permute-start(bf16[512,512]{1,0:T(8,128)(2,1)} %get-tuple-element.34), channel_id=1, source_target_pairs={{4,0},{6,2},{8,4},{10,6},{12,8},{14,10},{5,1},{7,3},{9,5},{11,7},{... | collective-permute-start | bytes 1572872 | tf_op jit(solution)/shard_map/ppermute | solution.py:547
  12.4 28.6 %collective-permute-start.6 = (bf16[1040,512]{1,0:T(8,128)(2,1)}, bf16[1040,512]{1,0:T(8,128)(2,1)}, u32[]{:S(2)}, u32[]{:S(2)}) collective-permute-start(bf16[1040,512]{1,0:T(8,128)(2,1)} %get-tuple-element.27), channel_id=1, source_target_pairs={{0,4},{2,6},{4,8},{6,10},{8,12},{10,14},{1,5},{3,7},{5,9},{7,11},{... | collective-permute-start | bytes 3194888 | tf_op jit(solution)/shard_map/ppermute | solution.py:547
  16.2 1.4 %copy-start.10 = (f32[1024,512]{1,0:T(8,128)}, f32[1024,512]{1,0:T(8,128)S(1)}, u32[]{:S(2)}) copy-start(f32[1024,512]{1,0:T(8,128)S(1)} %get-tuple-element.35.rest_0_) | copy-start | bytes 6291460
  17.6 1.4 %copy-start.12 = (f32[1024,512]{1,0:T(8,128)}, f32[1024,512]{1,0:T(8,128)S(1)}, u32[]{:S(2)}) copy-start(f32[1024,512]{1,0:T(8,128)S(1)} %get-tuple-element.36.rest_1_) | copy-start | bytes 6291460
  19.0 1.4 %copy-start.14 = (f32[1024,512]{1,0:T(8,128)}, f32[1024,512]{1,0:T(8,128)S(1)}, u32[]{:S(2)}) copy-start(f32[1024,512]{1,0:T(8,128)S(1)} %get-tuple-element.37.rest_2_) | copy-start | bytes 6291460
  22.6 1.3 %copy-start.4 = (f32[1024,512]{1,0:T(8,128)}, f32[1024,512]{1,0:T(8,128)S(1)}, u32[]{:S(2)}) copy-start(f32[1024,512]{1,0:T(8,128)S(1)} %get-tuple-element.28.rest_0_) | copy-start | bytes 6291460
  23.9 1.4 %copy-start.6 = (f32[1024,512]{1,0:T(8,128)}, f32[1024,512]{1,0:T(8,128)S(1)}, u32[]{:S(2)}) copy-start(f32[1024,512]{1,0:T(8,128)S(1)} %get-tuple-element.29.rest_1_) | copy-start | bytes 6291460
  25.2 1.3 %copy-start.8 = (f32[1024,512]{1,0:T(8,128)}, f32[1024,512]{1,0:T(8,128)S(1)}, u32[]{:S(2)}) copy-start(f32[1024,512]{1,0:T(8,128)S(1)} %get-tuple-element.30.rest_2_) | copy-start | bytes 6291460
  26.6 14.4 %copy-start.3 = (bf16[1024,1024]{1,0:T(8,128)(2,1)S(1)}, bf16[1024,1024]{1,0:T(8,128)(2,1)}, u32[]{:S(2)}) copy-start(bf16[1024,1024]{1,0:T(8,128)(2,1)} %q.13) | copy-start | bytes 6291460
  28.6 37.5 %collective-permute-start.8 = (bf16[512,512]{1,0:T(8,128)(2,1)S(1)}, bf16[512,512]{1,0:T(8,128)(2,1)S(1)}, u32[]{:S(2)}, u32[]{:S(2)}) collective-permute-start(bf16[512,512]{1,0:T(8,128)(2,1)S(1)} %broadcast_select_fusion.1), channel_id=1, source_target_pairs={{0,2},{2,0},{4,6},{6,4},{8,10},{10,8},{12,14},{14,12},{1,3},{3,1},... | collective-permute-start | bytes 1572872 | tf_op jit(solution)/shard_map/ppermute | solution.py:547
  33.8 35.0 %collective-permute-start.1 = (bf16[512,512]{1,0:T(8,128)(2,1)}, bf16[512,512]{1,0:T(8,128)(2,1)S(1)}, u32[]{:S(2)}, u32[]{:S(2)}) collective-permute-start(bf16[512,512]{1,0:T(8,128)(2,1)} %collective-permute-done.pb), channel_id=1, source_target_pairs={{0,4},{4,8},{8,12},{1,5},{5,9},{9,13},{16,20},{20,24},{24,28},{17,... | collective-permute-start | bytes 1572872 | tf_op jit(solution)/shard_map/ppermute | solution.py:547
  35.2 19.8 %collective-permute-start.5 = (bf16[520,512]{1,0:T(8,128)(2,1)S(1)}, bf16[520,512]{1,0:T(8,128)(2,1)S(1)}, u32[]{:S(2)}, u32[]{:S(2)}) collective-permute-start(bf16[520,512]{1,0:T(8,128)(2,1)S(1)} %broadcast_select_fusion), channel_id=1, source_target_pairs={{0,2},{2,0},{4,6},{6,4},{8,10},{10,8},{12,14},{14,12},{1,3},{3,1},... | collective-permute-start | bytes 1597448 | tf_op jit(solution)/shard_map/ppermute | solution.py:547
  36.2 25.1 %collective-permute-start.3 = (bf16[520,512]{1,0:T(8,128)(2,1)}, bf16[520,512]{1,0:T(8,128)(2,1)S(1)}, u32[]{:S(2)}, u32[]{:S(2)}) collective-permute-start(bf16[520,512]{1,0:T(8,128)(2,1)} %collective-permute-done.2.pa.pb), channel_id=1, source_target_pairs={{0,4},{4,8},{8,12},{1,5},{5,9},{9,13},{16,20},{20,24},{24,28},{17,... | collective-permute-start | bytes 1597448 | tf_op jit(solution)/shard_map/ppermute | solution.py:547
  41.0 1.6 %copy-start.11 = (f32[1024,512]{1,0:T(8,128)S(1)}, f32[1024,512]{1,0:T(8,128)}, u32[]{:S(2)}) copy-start(f32[1024,512]{1,0:T(8,128)} %copy-done.10) | copy-start | bytes 6291460
  42.6 1.6 %copy-start.13 = (f32[1024,512]{1,0:T(8,128)S(1)}, f32[1024,512]{1,0:T(8,128)}, u32[]{:S(2)}) copy-start(f32[1024,512]{1,0:T(8,128)} %copy-done.12) | copy-start | bytes 6291460
  44.2 1.6 %copy-start.15 = (f32[1024,512]{1,0:T(8,128)S(1)}, f32[1024,512]{1,0:T(8,128)}, u32[]{:S(2)}) copy-start(f32[1024,512]{1,0:T(8,128)} %copy-done.14) | copy-start | bytes 6291460
  45.8 4.1 %copy-start.5 = (f32[1024,512]{1,0:T(8,128)S(1)}, f32[1024,512]{1,0:T(8,128)}, u32[]{:S(2)}) copy-start(f32[1024,512]{1,0:T(8,128)} %copy-done.4) | copy-start | bytes 6291460
  45.8 4.1 %copy-start.7 = (f32[1024,512]{1,0:T(8,128)S(1)}, f32[1024,512]{1,0:T(8,128)}, u32[]{:S(2)}) copy-start(f32[1024,512]{1,0:T(8,128)} %copy-done.6) | copy-start | bytes 6291460
  45.8 4.1 %copy-start.9 = (f32[1024,512]{1,0:T(8,128)S(1)}, f32[1024,512]{1,0:T(8,128)}, u32[]{:S(2)}) copy-start(f32[1024,512]{1,0:T(8,128)} %copy-done.8) | copy-start | bytes 6291460
where the time goes:
time: 72.1 us; the launch traced here: 71.7 us
  Pallas kernels  27.5 us (38%)
  waiting for transfers between devices  15.5 us (21%)
  starting transfers between devices  14 us (19%)
  local copies, waits for them, and re-layouts  12.9 us (18%)
  other arithmetic  1.37 us (2%)
    ppermute x9, waiting for transfers between devices, send(): return lax.ppermute(x, 'seq', route)  15.5 us
    ppermute x9, starting transfers between devices, send(): return lax.ppermute(x, 'seq', route)  14 us
    unnamed x34, local copies, waits for them, and re-layouts  12.9 us
    pallas_call x2, Pallas kernels, far(): pl.pallas_call(functools.partial(far_kernel, h, n), out_shape=(STATE,) *...  8.08 us
    pallas_call x2, Pallas kernels, second_pair(): pl.pallas_call(functools.partial(second_pair_kernel, role, n), out_shape=...  5.42 us
    pallas_call x1, Pallas kernels, first_pair(): pl.pallas_call(functools.partial(first_pair_kernel, n), out_shape=(jax.Sh...  4.8 us
    pallas_call x2, Pallas kernels, own(): pl.pallas_call(functools.partial(own_kernel, h), out_shape=(STATE,) * 3,...  4.46 us
    pallas_call x1, Pallas kernels, pack_rest(): pl.pallas_call(pack_rest_kernel, out_shape=tuple((jax.ShapeDtypeStruct((r...  2.41 us
  transfers between devices with their start and end apart: 9, of which 5 were waited for; matrix products, arithmetic and copies ran while one was open for 2% of the time, Pallas kernels for 31%

commit v1 on v0

--- a/solution.py
+++ b/solution.py
@@ -113,13 +113,32 @@
     )(k, v, ids)
 
 
-def pack_rest_kernel(k, v, ids, b1, f2, b2, ids_v, stage, sem, ids_sem, out_sem):
+def head_copies(k, v, head, target, sem):
+    return [
+        pltpu.make_async_copy(
+            src.at[pl.ds(0, HALF), pl.ds(head * HEAD_DIM, HEAD_DIM)],
+            target.at[:, pl.ds(part * HEAD_DIM, HEAD_DIM)],
+            sem.at[part],
+        )
+        for part, src in enumerate((k, v))
+    ]
+
+
+def pack_rest_kernel(k, v, ids, b1, f2, f3, b2, ids_v, stage, sem, ids_sem, out_sem):
     get_ids = pltpu.make_async_copy(ids, ids_v, ids_sem)
     get_ids.start()
-    pieces = ((1, 0, b1), (0, 1, f2), (1, 1, b2))
+    whole = pl.ds(0, HALF)
+    areas = [
+        stage.at[0, pl.ds(0, HALF + 8)],
+        stage.at[1, whole, pl.ds(0, 2 * HEAD_DIM)],
+        stage.at[2, whole, pl.ds(0, 2 * HEAD_DIM)],
+        stage.at[3, whole],
+    ]
     copies = [
-        block_copies(k, v, role, h, stage.at[i, pl.ds(0, HALF)], sem.at[i])
-        for i, (role, h, _) in enumerate(pieces)
+        block_copies(k, v, 1, 0, stage.at[0, whole], sem.at[0]),
+        head_copies(k, v, PAIR, areas[1], sem.at[1]),
+        head_copies(k, v, PAIR + 1, areas[2], sem.at[2]),
+        block_copies(k, v, 1, 1, areas[3], sem.at[3]),
     ]
     for pair in copies:
         for copy in pair:
@@ -127,30 +146,33 @@
     get_ids.wait()
     stage[0, HALF:SECOND, :] = ids_row(ids_v, 1)
     sends = []
-    for i, (_, _, piece) in enumerate(pieces):
+    for i, piece in enumerate((b1, f2, f3, b2)):
         for copy in copies[i]:
             copy.wait()
-        rows = pl.ds(0, HALF + 8 if i == 0 else HALF)
-        sends.append(pltpu.make_async_copy(stage.at[i, rows], piece, out_sem.at[i]))
+        sends.append(pltpu.make_async_copy(areas[i], piece, out_sem.at[i]))
         sends[-1].start()
     for send in sends:
         send.wait()
 
 
 def pack_rest(k, v, ids):
+    shapes = (
+        (HALF + 8, HALF),
+        (HALF, 2 * HEAD_DIM),
+        (HALF, 2 * HEAD_DIM),
+        (HALF, HALF),
+    )
     return pl.pallas_call(
         pack_rest_kernel,
-        out_shape=tuple(
-            jax.ShapeDtypeStruct((r, HALF), jnp.bfloat16) for r in (HALF + 8, HALF, HALF)
-        ),
+        out_shape=tuple(jax.ShapeDtypeStruct(x, jnp.bfloat16) for x in shapes),
         in_specs=[HBM] * 3,
-        out_specs=[HBM] * 3,
+        out_specs=[HBM] * 4,
         scratch_shapes=[
             pltpu.VMEM((1, 2 * HALF), jnp.int32),
-            pltpu.VMEM((3, SECOND, HALF), jnp.bfloat16),
-            pltpu.SemaphoreType.DMA((3, 2)),
+            pltpu.VMEM((4, SECOND, HALF), jnp.bfloat16),
+            pltpu.SemaphoreType.DMA((4, 2)),
             pltpu.SemaphoreType.DMA,
-            pltpu.SemaphoreType.DMA((3,)),
+            pltpu.SemaphoreType.DMA((4,)),
         ],
         compiler_params=PARAMS,
         cost_estimate=pl.CostEstimate(
@@ -285,7 +307,13 @@
     )(q, k, v, hot)
 
 
-def far_kernel(h, n, idx, q, hot, zp, za, zb, pa, pb, *rest):
+def by_head(first, second):
+    return [
+        x.at[:, pl.ds(part * HEAD_DIM, HEAD_DIM)] for part in range(2) for x in (first, second)
+    ]
+
+
+def far_kernel(h, n, idx, q, hot, zp, za, zb, pa, pb2, pb3, *rest):
     (acc0, mx0, ls0), (acc, mx, ls) = rest[:3], rest[3:6]
     far, seg, sem, seg_sem = rest[6:]
     from_partner = idx[0] >= n - 2
@@ -300,14 +328,18 @@
     pair = pl.ds(h * SECOND, HALF)
     whole = pl.ds(0, HALF)
     back = (za.at[whole], zb)[h]
-    partner = (pa.at[whole], pb)[h]
     fetch_ids(0, zp.at[id_rows]).start()
     fetch(0, zp.at[pair]).start()
 
     @pl.when(from_partner)
     def _():
         fetch_ids(1, pa.at[id_rows]).start()
-        fetch(1, partner).start()
+        if h == 0:
+            fetch(1, pa.at[whole]).start()
+        else:
+            for j, src in enumerate(by_head(pb2, pb3)):
+                to = far.at[1, :, pl.ds(j * HEAD_DIM, HEAD_DIM)]
+                pltpu.make_async_copy(src, to, sem.at[1]).start()
 
     @pl.when(jnp.logical_not(from_partner))
     def _():
@@ -338,11 +370,11 @@
                 mx[rows, cols] = tops[i][mine]
 
 
-def far(h, n, idx, q, hot, zp, za, zb, pa, pb, state):
+def far(h, n, idx, q, hot, zp, za, zb, pa, pb2, pb3, state):
     return pl.pallas_call(
         functools.partial(far_kernel, h, n),
         out_shape=(STATE,) * 3,
-        in_specs=[SMEM] + [VMEM] * 2 + [ANY] * 5 + [VMEM] * 3,
+        in_specs=[SMEM] + [VMEM] * 2 + [ANY] * 6 + [VMEM] * 3,
         out_specs=[VMEM] * 3,
         scratch_shapes=[
             pltpu.VMEM((2, HALF, HALF), jnp.bfloat16),
@@ -352,17 +384,20 @@
         ],
         compiler_params=PARAMS,
         cost_estimate=cost(5),
-    )(idx, q, hot, zp, za, zb, pa, pb, *state)
-
-
-def finish(h, role, q, hot, piece, hot_mid, state, out, o_buf, out_sem):
+    )(idx, q, hot, zp, za, zb, pa, pb2, pb3, *state)
+
+
+BOTH = ((0, 0, PAIR), (1, 1, PAIR + 1))
+
+
+def finish(h, role, q, hot, piece, hot_mid, state, out, o_buf, out_sem, heads=BOTH):
     acc, mx, ls = state
     base = role * HALF
     sends = []
-    for g in range(PAIR):
+    for g, k_at, v_at in heads:
         q2 = stacked_queries(q, hot, base, (PAIR * h + g) * GROUPS)
-        k_aug = jnp.concatenate([piece[0:HALF, head_cols(g)], hot_mid], axis=1)
-        v_aug = with_ones(piece[0:HALF, head_cols(PAIR + g)])
+        k_aug = jnp.concatenate([piece[0:HALF, head_cols(k_at)], hot_mid], axis=1)
+        v_aug = with_ones(piece[0:HALF, head_cols(v_at)])
         for t in range(TILES):
             s = dot_nt(tile_rows(q2, t), k_aug)
             old = load_state(mx, base, g)[t]
@@ -390,7 +425,7 @@
 
 
 def first_pair_kernel(
-    n, idx, q, hot, r1, pa, pb, d1, f1, k, v, *rest
+    n, idx, q, hot, r1, pa, pb2, pb3, d1, f1, k, v, *rest
 ):
     state1, state2 = rest[:3], rest[3:6]
     out, hots, mid, seg, sem, extra, extra_sem, o_buf, out_sem = rest[6:]
@@ -413,7 +448,11 @@
 
     def fetch_extra(role, srcs):
         return [
-            pltpu.make_async_copy(src, extra.at[role, :, cols[i]], extra_sem.at[role, i])
+            pltpu.make_async_copy(
+                src,
+                extra.at[role, :, pl.ds(i * HEAD_DIM, HEAD_DIM)],
+                extra_sem.at[role, i],
+            )
             for i, src in enumerate(srcs)
         ]
 
@@ -423,10 +462,14 @@
         def _():
             if role == 0:
                 fetch(role, here, columns(here))
-                srcs = columns(pb)
+                srcs = by_head(pb2, pb3)
             else:
                 fetch(role, f1, own_front(0))
-                srcs = own_front(1)
+                srcs = [
+                    x.at[whole, pl.ds(head * HEAD_DIM, HEAD_DIM)]
+                    for x in (k, v)
+                    for head in (PAIR, PAIR + 1)
+                ]
             for copy in fetch_extra(role, srcs):
                 copy.start()
 
@@ -465,7 +508,7 @@
 
         @pl.when(local)
         def _():
-            for copy in fetch_extra(role, columns(pb)):
+            for copy in fetch_extra(role, by_head(pb2, pb3)):
                 copy.wait()
             for copy in finish(
                 1, role, q, hot, extra.at[role], hots[role], state2, out, o_buf, out_sem
@@ -494,7 +537,7 @@
             pltpu.VMEM((2, 8, HALF), jnp.bfloat16),
             pltpu.SemaphoreType.DMA((2, 3)),
             piece,
-            pltpu.SemaphoreType.DMA((2, 2)),
+            pltpu.SemaphoreType.DMA((2, 4)),
             *OUT_SCRATCH,
         ],
         compiler_params=PARAMS,
@@ -503,32 +546,52 @@
     )(idx, q, hot, *pieces, *state1, *state2)
 
 
-def second_pair_kernel(role, n, idx, q, hot, piece, hots, acc, mx, ls, _, out, o_buf, out_sem):
-    if role == 0:
-        needed = (idx[0] % 2 == 0) & (idx[0] > 0)
+ALONE = (((0, 0, 1),), ((1, 0, 1),))
+
+
+def second_pair_kernel(n, idx, q, hot, *rest):
+    *pieces, hots, acc, mx, ls, _, out, o_buf, out_sem = rest
+    relayed = (idx[0] % 2 == 0) & (idx[0] > 0)
+
+    def go(jobs):
+        copies = []
+        for role, piece, heads in jobs:
+            copies += finish(
+                1, role, q, hot, piece, hots[role], (acc, mx, ls), out, o_buf, out_sem, heads
+            )
+        for copy in copies:
+            copy.wait()
+
+    if len(pieces) == 1:
+
+        @pl.when(relayed)
+        def _():
+            go([(0, pieces[0], ALONE[1])])
+
     else:
-        needed = idx[0] < n - 1
-
-    @pl.when(needed)
-    def _():
-        state = (acc, mx, ls)
-        for copy in finish(
-            1, role, q, hot, piece, hots[role], state, out, o_buf, out_sem
-        ):
-            copy.wait()
-
-
-def second_pair(role, n, idx, q, hot, piece, hots, state, out):
+        front, back = pieces
+
+        @pl.when(relayed)
+        def _():
+            go([(1, back, BOTH), (0, front, ALONE[0])])
+
+        @pl.when(jnp.logical_not(relayed) & (idx[0] < n - 1))
+        def _():
+            go([(1, back, BOTH)])
+
+
+def second_pair(n, idx, q, hot, pieces, hots, state, out):
+    count = len(pieces)
     return pl.pallas_call(
-        functools.partial(second_pair_kernel, role, n),
+        functools.partial(second_pair_kernel, n),
         out_shape=jax.ShapeDtypeStruct(q.shape, q.dtype),
-        in_specs=[SMEM] + [VMEM] * 7 + [ANY],
+        in_specs=[SMEM] + [VMEM] * (count + 6) + [ANY],
         out_specs=ANY,
-        input_output_aliases={8: 0},
+        input_output_aliases={count + 7: 0},
         scratch_shapes=OUT_SCRATCH,
         compiler_params=PARAMS,
         cost_estimate=cost(5),
-    )(idx, q, hot, piece, hots, *state, out)
+    )(idx, q, hot, *pieces, hots, *state, out)
 
 
 def body(queries, key_states, value_states, segment_ids):
@@ -554,9 +617,10 @@
     f1, front = pack_front(*in_hbm)
     pa = send(f1, partner)
     zp = send(front, up_two)
-    b1, f2, b2 = pack_rest(*in_hbm)
+    b1, f2, f3, b2 = pack_rest(*in_hbm)
     za = send(b1, down_two)
-    pb = send(f2, partner)
+    pb2 = send(f2, partner)
+    pb3 = send(f3, partner)
     zb = send(b2, down_two)
     state1 = own(0, q, k, v, hot)
     r1 = send(pa, relay)
@@ -564,16 +628,17 @@
     even = seq % 2 == 0
     back = jnp.where(even, za, b1)
     d1 = send(back, partner)
-    r2 = send(pb, relay)
-    state1 = far(0, n, idx, q, hot, zp, za, za, pa, pa, state1)
+    r2 = send(pb2, relay)
+    state1 = far(0, n, idx, q, hot, zp, za, za, pa, pa, pa, state1)
     back = jnp.where(even, zb, b2)
     d2 = send(back, partner)
-    state2 = far(1, n, idx, q, hot, zp, za, zb, pa, pb, state2)
-
-    pieces = (r1, pa, pb, d1, f1, k, v)
+    state2 = far(1, n, idx, q, hot, zp, za, zb, pa, pb2, pb3, state2)
+
+    r3 = send(pb3, relay)
+    pieces = (r1, pa, pb2, pb3, d1, f1, k, v)
     out, hots = first_pair(n, idx, q, hot, pieces, state1, state2)
-    out = second_pair(1, n, idx, q, hot, d2, hots, state2, out)
-    return second_pair(0, n, idx, q, hot, r2, hots, state2, out)
+    out = second_pair(n, idx, q, hot, (r2, d2), hots, state2, out)
+    return second_pair(n, idx, q, hot, (r3,), hots, state2, out)
 
 
 def solution(mesh):

time: 72.1 us -> 76.7 us (1.064)
  the two profiles are of different devices: /device:TPU:24 before, /device:TPU:0 now
where the time goes in v1:
time: 76.7 us; the launch traced here: 76 us
  starting transfers between devices  27.2 us (35%)
  Pallas kernels  25.3 us (33%)
  local copies, waits for them, and re-layouts  12.9 us (17%)
  waiting for transfers between devices  8.73 us (11%)
  other arithmetic  1.38 us (2%)
    ppermute x11, starting transfers between devices, send(): return lax.ppermute(x, 'seq', route)  27.2 us
    unnamed x38, local copies, waits for them, and re-layouts  12.9 us
    ppermute x11, waiting for transfers between devices, send(): return lax.ppermute(x, 'seq', route)  8.73 us
    pallas_call x2, Pallas kernels, far(): pl.pallas_call(functools.partial(far_kernel, h, n), out_shape=(STATE,) *...  7.69 us
    pallas_call x1, Pallas kernels, first_pair(): pl.pallas_call(functools.partial(first_pair_kernel, n), out_shape=(jax.Sh...  5.45 us
    pallas_call x2, Pallas kernels, own(): pl.pallas_call(functools.partial(own_kernel, h), out_shape=(STATE,) * 3,...  4.6 us
    pallas_call x2, Pallas kernels, second_pair(): pl.pallas_call(functools.partial(second_pair_kernel, n), out_shape=jax.Sh...  2.74 us
    pallas_call x1, Pallas kernels, pack_rest(): pl.pallas_call(pack_rest_kernel, out_shape=tuple((jax.ShapeDtypeStruct(x,...  2.43 us
  transfers between devices with their start and end apart: 11, of which 2 were waited for; matrix products, arithmetic and copies ran while one was open for 2% of the time, Pallas kernels for 30%

profile of v1, /device:TPU:0, one launch (start us, length us, event | category | flops | bytes accessed | tf_op | source)
XLA Modules:
  0.0 76.0 jit_solution(10831150632954888818)
XLA Ops:
  0.0 2.4 %pack1.1 = (bf16[520,512]{1,0:T(8,128)(2,1)S(1)}, bf16[512,256]{1,0:T(8,128)(2,1)}, bf16[512,256]{1,0:T(8,128)(2,1)S(1)}, bf16[512,512]{1,0:T(8,128)(2,1)}) custom-call(bf16[1024,512]{1,0:T(8,128)(2,1)} %k.9, bf16[1024,512]{1,0:T(8,128)(2,1)} %v.9, s32[1,1024]{1,0:T(1,128)} %bitcast.2), custom_call_target="tpu_custom_call" | custom-call | flops 1048576 | bytes 3145728 | tf_op jit(solution)/shard_map/pack1/pallas_call | solution.py:165
  2.5 1.3 %collective-permute-start.5 = (bf16[520,512]{1,0:T(8,128)(2,1)S(1)}, bf16[520,512]{1,0:T(8,128)(2,1)S(1)}, u32[]{:S(2)}, u32[]{:S(2)}) collective-permute-start(bf16[520,512]{1,0:T(8,128)(2,1)S(1)} %get-tuple-element.28), channel_id=1, source_target_pairs={{4,0},{6,2},{8,4},{10,6},{12,8},{14,10},{5,1},{7,3},{9,5},{11,7},{... | collective-permute-start | bytes 1597448 | tf_op jit(solution)/shard_map/ppermute | solution.py:610
  3.8 2.4 %pack0.1 = (bf16[520,512]{1,0:T(8,128)(2,1)}, bf16[1040,512]{1,0:T(8,128)(2,1)}) custom-call(bf16[1024,512]{1,0:T(8,128)(2,1)} %k.9, bf16[1024,512]{1,0:T(8,128)(2,1)} %v.9, s32[1,1024]{1,0:T(1,128)} %bitcast.3), custom_call_target="tpu_custom_call" | custom-call | flops 1048576 | bytes 2097152 | tf_op jit(solution)/shard_map/pack0/pallas_call | solution.py:94
  6.1 3.1 %collective-permute-start.2 = (bf16[520,512]{1,0:T(8,128)(2,1)}, bf16[520,512]{1,0:T(8,128)(2,1)}, u32[]{:S(2)}, u32[]{:S(2)}) collective-permute-start(bf16[520,512]{1,0:T(8,128)(2,1)} %get-tuple-element.26.f1), channel_id=1, source_target_pairs={{0,2},{2,0},{4,6},{6,4},{8,10},{10,8},{12,14},{14,12},{1,3},{3,1},... | collective-permute-start | bytes 1597448 | tf_op jit(solution)/shard_map/ppermute | solution.py:610
  9.2 1.3 %collective-permute-start.8 = (bf16[512,512]{1,0:T(8,128)(2,1)}, bf16[512,512]{1,0:T(8,128)(2,1)}, u32[]{:S(2)}, u32[]{:S(2)}) collective-permute-start(bf16[512,512]{1,0:T(8,128)(2,1)} %get-tuple-element.36), channel_id=1, source_target_pairs={{4,0},{6,2},{8,4},{10,6},{12,8},{14,10},{5,1},{7,3},{9,5},{11,7},{... | collective-permute-start | bytes 1572872 | tf_op jit(solution)/shard_map/ppermute | solution.py:610
  10.5 0.1 collective-permute-start
  10.6 6.2 %collective-permute-start.7 = (bf16[1040,512]{1,0:T(8,128)(2,1)}, bf16[1040,512]{1,0:T(8,128)(2,1)}, u32[]{:S(2)}, u32[]{:S(2)}) collective-permute-start(bf16[1040,512]{1,0:T(8,128)(2,1)} %get-tuple-element.29), channel_id=1, source_target_pairs={{0,4},{2,6},{4,8},{6,10},{8,12},{10,14},{1,5},{3,7},{5,9},{7,11},{... | collective-permute-start | bytes 3194888 | tf_op jit(solution)/shard_map/ppermute | solution.py:610
  16.8 0.2 fusion.hot
  17.0 2.3 %shard_map.48 = (f32[1024,512]{1,0:T(8,128)S(1)}, f32[1024,512]{1,0:T(8,128)S(1)}, f32[1024,512]{1,0:T(8,128)S(1)}) custom-call(bf16[1024,1024]{1,0:T(8,128)(2,1)S(1)} %copy-done.2, bf16[1024,512]{1,0:T(8,128)(2,1)S(1)} %copy-done, bf16[1024,512]{1,0:T(8,128)(2,1)S(1)} %copy-done.1, bf16[1024,128]{1,0:T(8,128)(2,1)S(1)} %fusion.hot), custom_call_target="tpu_custom_call" | custom-call | flops 5368709120 | bytes 8388608 | tf_op jit(solution)/shard_map/pallas_call | solution.py:300
  19.3 1.3 %copy-done.12 = f32[1024,512]{1,0:T(8,128)} copy-done((f32[1024,512]{1,0:T(8,128)}, f32[1024,512]{1,0:T(8,128)S(1)}, u32[]{:S(2)}) %copy-start.12) | copy-done | bytes 2097176
  20.7 1.3 %copy-done.14 = f32[1024,512]{1,0:T(8,128)} copy-done((f32[1024,512]{1,0:T(8,128)}, f32[1024,512]{1,0:T(8,128)S(1)}, u32[]{:S(2)}) %copy-start.14) | copy-done | bytes 2097176
  22.0 1.4 %copy-done.16 = f32[1024,512]{1,0:T(8,128)} copy-done((f32[1024,512]{1,0:T(8,128)}, f32[1024,512]{1,0:T(8,128)S(1)}, u32[]{:S(2)}) %copy-start.16) | copy-done | bytes 2097176
  23.4 3.7 %collective-permute-done.pb3 = bf16[512,256]{1,0:T(8,128)(2,1)S(1)} collective-permute-done((bf16[512,256]{1,0:T(8,128)(2,1)S(1)}, bf16[512,256]{1,0:T(8,128)(2,1)S(1)}, u32[]{:S(2)}, u32[]{:S(2)}) %collective-permute-start) | collective-permute-done | bytes 262176 | tf_op jit(solution)/shard_map/ppermute | solution.py:610
  27.1 1.7 %collective-permute-start.4 = (bf16[512,256]{1,0:T(8,128)(2,1)}, bf16[512,256]{1,0:T(8,128)(2,1)}, u32[]{:S(2)}, u32[]{:S(2)}) collective-permute-start(bf16[512,256]{1,0:T(8,128)(2,1)} %get-tuple-element.27), channel_id=1, source_target_pairs={{0,2},{2,0},{4,6},{6,4},{8,10},{10,8},{12,14},{14,12},{1,3},{3,1},... | collective-permute-start | bytes 786440 | tf_op jit(solution)/shard_map/ppermute | solution.py:610
  28.9 2.3 %shard_map.46 = (f32[1024,512]{1,0:T(8,128)S(1)}, f32[1024,512]{1,0:T(8,128)S(1)}, f32[1024,512]{1,0:T(8,128)S(1)}) custom-call(bf16[1024,1024]{1,0:T(8,128)(2,1)S(1)} %copy-done.2, bf16[1024,512]{1,0:T(8,128)(2,1)S(1)} %copy-done, bf16[1024,512]{1,0:T(8,128)(2,1)S(1)} %copy-done.1, bf16[1024,128]{1,0:T(8,128)(2,1)S(1)} %fusion.hot), custom_call_target="tpu_custom_call" | custom-call | flops 5368709120 | bytes 8388608 | tf_op jit(solution)/shard_map/pallas_call | solution.py:300
  31.2 1.3 %copy-done.6 = f32[1024,512]{1,0:T(8,128)} copy-done((f32[1024,512]{1,0:T(8,128)}, f32[1024,512]{1,0:T(8,128)S(1)}, u32[]{:S(2)}) %copy-start.6) | copy-done | bytes 2097176
  32.5 1.4 %copy-done.8 = f32[1024,512]{1,0:T(8,128)} copy-done((f32[1024,512]{1,0:T(8,128)}, f32[1024,512]{1,0:T(8,128)S(1)}, u32[]{:S(2)}) %copy-start.8) | copy-done | bytes 2097176
  33.9 1.4 %copy-done.10 = f32[1024,512]{1,0:T(8,128)} copy-done((f32[1024,512]{1,0:T(8,128)}, f32[1024,512]{1,0:T(8,128)S(1)}, u32[]{:S(2)}) %copy-start.10) | copy-done | bytes 2097176
  35.3 4.4 %collective-permute-start.9 = (bf16[512,256]{1,0:T(8,128)(2,1)}, bf16[512,256]{1,0:T(8,128)(2,1)S(1)}, u32[]{:S(2)}, u32[]{:S(2)}) collective-permute-start(bf16[512,256]{1,0:T(8,128)(2,1)} %collective-permute-done.4.pb2), channel_id=1, source_target_pairs={{0,4},{4,8},{8,12},{1,5},{5,9},{9,13},{16,20},{20,24},{24,28},{17,... | collective-permute-start | bytes 786440 | tf_op jit(solution)/shard_map/ppermute | solution.py:610
  39.7 3.5 %collective-permute-start.1 = (bf16[512,256]{1,0:T(8,128)(2,1)}, bf16[512,256]{1,0:T(8,128)(2,1)S(1)}, u32[]{:S(2)}, u32[]{:S(2)}) collective-permute-start(bf16[512,256]{1,0:T(8,128)(2,1)} %copy-done.4), channel_id=1, source_target_pairs={{0,4},{4,8},{8,12},{1,5},{5,9},{9,13},{16,20},{20,24},{24,28},{17,... | collective-permute-start | bytes 786440 | tf_op jit(solution)/shard_map/ppermute | solution.py:610
  43.2 1.1 %broadcast_select_fusion.1 = bf16[512,512]{1,0:T(8,128)(2,1)S(1)} fusion(bf16[512,512]{1,0:T(8,128)(2,1)} %collective-permute-done.8.zb, bf16[512,512]{1,0:T(8,128)(2,1)} %get-tuple-element.36, pred[]{:T(512)S(6)} %eq.21), kind=kLoop, calls=%fused_computation.3 | loop fusion | flops 262144 | bytes 1572865 | tf_op jit(solution)/shard_map/jit(_where)/select_n | solution.py:633
  44.3 0.1 collective-permute-start.10
  44.5 2.1 %collective-permute-start.6 = (bf16[520,512]{1,0:T(8,128)(2,1)S(1)}, bf16[520,512]{1,0:T(8,128)(2,1)S(1)}, u32[]{:S(2)}, u32[]{:S(2)}) collective-permute-start(bf16[520,512]{1,0:T(8,128)(2,1)S(1)} %broadcast_select_fusion), channel_id=1, source_target_pairs={{0,2},{2,0},{4,6},{6,4},{8,10},{10,8},{12,14},{14,12},{1,3},{3,1},... | collective-permute-start | bytes 1597448 | tf_op jit(solution)/shard_map/ppermute | solution.py:610
  46.6 3.5 %collective-permute-start.3 = (bf16[520,512]{1,0:T(8,128)(2,1)}, bf16[520,512]{1,0:T(8,128)(2,1)S(1)}, u32[]{:S(2)}, u32[]{:S(2)}) collective-permute-start(bf16[520,512]{1,0:T(8,128)(2,1)} %collective-permute-done.2.pa.pb2.pb3), channel_id=1, source_target_pairs={{0,4},{4,8},{8,12},{1,5},{5,9},{9,13},{16,20},{20,24},{24,28},{17,... | collective-permute-start | bytes 1597448 | tf_op jit(solution)/shard_map/ppermute | solution.py:610
  50.1 1.6 %copy-done.13 = f32[1024,512]{1,0:T(8,128)S(1)} copy-done((f32[1024,512]{1,0:T(8,128)S(1)}, f32[1024,512]{1,0:T(8,128)}, u32[]{:S(2)}) %copy-start.13) | copy-done | bytes 2097176
  51.7 1.6 %copy-done.15 = f32[1024,512]{1,0:T(8,128)S(1)} copy-done((f32[1024,512]{1,0:T(8,128)S(1)}, f32[1024,512]{1,0:T(8,128)}, u32[]{:S(2)}) %copy-start.15) | copy-done | bytes 2097176
  53.3 1.6 %copy-done.17 = f32[1024,512]{1,0:T(8,128)S(1)} copy-done((f32[1024,512]{1,0:T(8,128)S(1)}, f32[1024,512]{1,0:T(8,128)}, u32[]{:S(2)}) %copy-start.17) | copy-done | bytes 2097176
  54.9 4.0 %shard_map.49 = (f32[1024,512]{1,0:T(8,128)S(1)}, f32[1024,512]{1,0:T(8,128)S(1)}, f32[1024,512]{1,0:T(8,128)S(1)}) custom-call(s32[1]{0:T(128)} %bitcast.idx, bf16[1024,1024]{1,0:T(8,128)(2,1)S(1)} %copy-done.3, bf16[1024,128]{1,0:T(8,128)(2,1)S(1)} %fusion.hot, bf16[1040,512]{1,0:T(8,128)(2,1)} %collective-permute-done.7.zp, ...), custom_call_target="tpu_custom_call" | custom-call | flops 5368709120 | bytes 8388608 | tf_op jit(solution)/shard_map/pallas_call | solution.py:374
  58.9 3.7 %shard_map.47 = (f32[1024,512]{1,0:T(8,128)S(1)}, f32[1024,512]{1,0:T(8,128)S(1)}, f32[1024,512]{1,0:T(8,128)S(1)}) custom-call(s32[1]{0:T(128)} %bitcast.idx, bf16[1024,1024]{1,0:T(8,128)(2,1)S(1)} %copy-done.3, bf16[1024,128]{1,0:T(8,128)(2,1)S(1)} %fusion.hot, bf16[1040,512]{1,0:T(8,128)(2,1)} %collective-permute-done.7.zp, ...), custom_call_target="tpu_custom_call" | custom-call | flops 5368709120 | bytes 8388608 | tf_op jit(solution)/shard_map/pallas_call | solution.py:374
  62.6 5.0 %collective-permute-done.6.d1 = bf16[520,512]{1,0:T(8,128)(2,1)S(1)} collective-permute-done((bf16[520,512]{1,0:T(8,128)(2,1)S(1)}, bf16[520,512]{1,0:T(8,128)(2,1)S(1)}, u32[]{:S(2)}, u32[]{:S(2)}) %collective-permute-start.6) | collective-permute-done | bytes 532512 | tf_op jit(solution)/shard_map/ppermute | solution.py:610
  67.6 5.5 %last0.1 = (bf16[1024,1024]{1,0:T(8,128)(2,1)}, bf16[2,512,128]{2,1,0:T(8,128)(2,1)S(1)}) custom-call(s32[1]{0:T(128)} %bitcast.idx, bf16[1024,1024]{1,0:T(8,128)(2,1)S(1)} %copy-done.3, bf16[1024,128]{1,0:T(8,128)(2,1)S(1)} %fusion.hot, bf16[520,512]{1,0:T(8,128)(2,1)S(1)} %collective-permute-done.3.r1, bf16[520,512]{1,0:T(8,128)(2,1)} %collective-permute-done.2.pa.pb2.pb3, ...), custom_call_target="tpu_custom_call" | custom-call | flops 5368709120 | bytes 8388608 | tf_op jit(solution)/shard_map/last0/pallas_call | solution.py:527
  73.1 2.7 %shard_map.50.rest_5_ = bf16[1024,1024]{1,0:T(8,128)(2,1)} custom-call(s32[1]{0:T(128)} %bitcast.idx, bf16[1024,1024]{1,0:T(8,128)(2,1)S(1)} %copy-done.3, bf16[1024,128]{1,0:T(8,128)(2,1)S(1)} %fusion.hot, bf16[512,256]{1,0:T(8,128)(2,1)S(1)} %collective-permute-done.9.rest_0_, ...), custom_call_target="tpu_custom_call", output_to_operand_aliasing={{}: (9, {})} | custom-call | flops 5368709120 | bytes 8388608 | tf_op jit(solution)/shard_map/pallas_call | solution.py:585
  (41 shorter events, 0.2 us)
Async XLA Ops:
  0.0 16.8 %copy-start.18 = (s32[1024]{0:T(1024)S(1)}, s32[1024]{0:T(1024)}, u32[]{:S(2)}) copy-start(s32[1024]{0:T(1024)} %param.7) | copy-start | bytes 12292
  0.0 17.0 %copy-start = (bf16[1024,512]{1,0:T(8,128)(2,1)S(1)}, bf16[1024,512]{1,0:T(8,128)(2,1)}, u32[]{:S(2)}) copy-start(bf16[1024,512]{1,0:T(8,128)(2,1)} %k.9) | copy-start | bytes 3145732
  0.0 17.0 %copy-start.1 = (bf16[1024,512]{1,0:T(8,128)(2,1)S(1)}, bf16[1024,512]{1,0:T(8,128)(2,1)}, u32[]{:S(2)}) copy-start(bf16[1024,512]{1,0:T(8,128)(2,1)} %v.9) | copy-start | bytes 3145732
  0.0 17.0 %copy-start.2 = (bf16[1024,1024]{1,0:T(8,128)(2,1)S(1)}, bf16[1024,1024]{1,0:T(8,128)(2,1)}, u32[]{:S(2)}) copy-start(bf16[1024,1024]{1,0:T(8,128)(2,1)} %q.13) | copy-start | bytes 6291460
  2.5 41.9 %collective-permute-start.5 = (bf16[520,512]{1,0:T(8,128)(2,1)S(1)}, bf16[520,512]{1,0:T(8,128)(2,1)S(1)}, u32[]{:S(2)}, u32[]{:S(2)}) collective-permute-start(bf16[520,512]{1,0:T(8,128)(2,1)S(1)} %get-tuple-element.28), channel_id=1, source_target_pairs={{4,0},{6,2},{8,4},{10,6},{12,8},{14,10},{5,1},{7,3},{9,5},{11,7},{... | collective-permute-start | bytes 1597448 | tf_op jit(solution)/shard_map/ppermute | solution.py:610
  6.1 38.4 %collective-permute-start.2 = (bf16[520,512]{1,0:T(8,128)(2,1)}, bf16[520,512]{1,0:T(8,128)(2,1)}, u32[]{:S(2)}, u32[]{:S(2)}) collective-permute-start(bf16[520,512]{1,0:T(8,128)(2,1)} %get-tuple-element.26.f1), channel_id=1, source_target_pairs={{0,2},{2,0},{4,6},{6,4},{8,10},{10,8},{12,14},{14,12},{1,3},{3,1},... | collective-permute-start | bytes 1597448 | tf_op jit(solution)/shard_map/ppermute | solution.py:610
  9.2 30.5 %collective-permute-start.8 = (bf16[512,512]{1,0:T(8,128)(2,1)}, bf16[512,512]{1,0:T(8,128)(2,1)}, u32[]{:S(2)}, u32[]{:S(2)}) collective-permute-start(bf16[512,512]{1,0:T(8,128)(2,1)} %get-tuple-element.36), channel_id=1, source_target_pairs={{4,0},{6,2},{8,4},{10,6},{12,8},{14,10},{5,1},{7,3},{9,5},{11,7},{... | collective-permute-start | bytes 1572872 | tf_op jit(solution)/shard_map/ppermute | solution.py:610
  10.5 16.6 %collective-permute-start = (bf16[512,256]{1,0:T(8,128)(2,1)S(1)}, bf16[512,256]{1,0:T(8,128)(2,1)S(1)}, u32[]{:S(2)}, u32[]{:S(2)}) collective-permute-start(bf16[512,256]{1,0:T(8,128)(2,1)S(1)} %get-tuple-element.25), channel_id=1, source_target_pairs={{0,2},{2,0},{4,6},{6,4},{8,10},{10,8},{12,14},{14,12},{1,3},{3,1},... | collective-permute-start | bytes 786440 | tf_op jit(solution)/shard_map/ppermute | solution.py:610
  10.6 36.0 %collective-permute-start.7 = (bf16[1040,512]{1,0:T(8,128)(2,1)}, bf16[1040,512]{1,0:T(8,128)(2,1)}, u32[]{:S(2)}, u32[]{:S(2)}) collective-permute-start(bf16[1040,512]{1,0:T(8,128)(2,1)} %get-tuple-element.29), channel_id=1, source_target_pairs={{0,4},{2,6},{4,8},{6,10},{8,12},{10,14},{1,5},{3,7},{5,9},{7,11},{... | collective-permute-start | bytes 3194888 | tf_op jit(solution)/shard_map/ppermute | solution.py:610
  19.3 1.3 %copy-start.12 = (f32[1024,512]{1,0:T(8,128)}, f32[1024,512]{1,0:T(8,128)S(1)}, u32[]{:S(2)}) copy-start(f32[1024,512]{1,0:T(8,128)S(1)} %get-tuple-element.37.rest_0_) | copy-start | bytes 6291460
  20.7 1.3 %copy-start.14 = (f32[1024,512]{1,0:T(8,128)}, f32[1024,512]{1,0:T(8,128)S(1)}, u32[]{:S(2)}) copy-start(f32[1024,512]{1,0:T(8,128)S(1)} %get-tuple-element.38.rest_1_) | copy-start | bytes 6291460
  22.0 1.4 %copy-start.16 = (f32[1024,512]{1,0:T(8,128)}, f32[1024,512]{1,0:T(8,128)S(1)}, u32[]{:S(2)}) copy-start(f32[1024,512]{1,0:T(8,128)S(1)} %get-tuple-element.39.rest_2_) | copy-start | bytes 6291460
  27.1 4.0 %copy-start.4 = (bf16[512,256]{1,0:T(8,128)(2,1)}, bf16[512,256]{1,0:T(8,128)(2,1)S(1)}, u32[]{:S(2)}) copy-start(bf16[512,256]{1,0:T(8,128)(2,1)S(1)} %collective-permute-done.pb3) | copy-start | bytes 786436
  27.1 8.2 %collective-permute-start.4 = (bf16[512,256]{1,0:T(8,128)(2,1)}, bf16[512,256]{1,0:T(8,128)(2,1)}, u32[]{:S(2)}, u32[]{:S(2)}) collective-permute-start(bf16[512,256]{1,0:T(8,128)(2,1)} %get-tuple-element.27), channel_id=1, source_target_pairs={{0,2},{2,0},{4,6},{6,4},{8,10},{10,8},{12,14},{14,12},{1,3},{3,1},... | collective-permute-start | bytes 786440 | tf_op jit(solution)/shard_map/ppermute | solution.py:610
  31.2 1.3 %copy-start.6 = (f32[1024,512]{1,0:T(8,128)}, f32[1024,512]{1,0:T(8,128)S(1)}, u32[]{:S(2)}) copy-start(f32[1024,512]{1,0:T(8,128)S(1)} %get-tuple-element.30.rest_0_) | copy-start | bytes 6291460
  32.5 1.4 %copy-start.8 = (f32[1024,512]{1,0:T(8,128)}, f32[1024,512]{1,0:T(8,128)S(1)}, u32[]{:S(2)}) copy-start(f32[1024,512]{1,0:T(8,128)S(1)} %get-tuple-element.31.rest_1_) | copy-start | bytes 6291460
  33.9 1.4 %copy-start.10 = (f32[1024,512]{1,0:T(8,128)}, f32[1024,512]{1,0:T(8,128)S(1)}, u32[]{:S(2)}) copy-start(f32[1024,512]{1,0:T(8,128)S(1)} %get-tuple-element.32.rest_2_) | copy-start | bytes 6291460
  35.3 14.8 %copy-start.3 = (bf16[1024,1024]{1,0:T(8,128)(2,1)S(1)}, bf16[1024,1024]{1,0:T(8,128)(2,1)}, u32[]{:S(2)}) copy-start(bf16[1024,1024]{1,0:T(8,128)(2,1)} %q.13) | copy-start | bytes 6291460
  35.3 14.8 %copy-start.5 = (bf16[512,256]{1,0:T(8,128)(2,1)S(1)}, bf16[512,256]{1,0:T(8,128)(2,1)}, u32[]{:S(2)}) copy-start(bf16[512,256]{1,0:T(8,128)(2,1)} %copy-done.4) | copy-start | bytes 786436
  35.3 37.8 %collective-permute-start.9 = (bf16[512,256]{1,0:T(8,128)(2,1)}, bf16[512,256]{1,0:T(8,128)(2,1)S(1)}, u32[]{:S(2)}, u32[]{:S(2)}) collective-permute-start(bf16[512,256]{1,0:T(8,128)(2,1)} %collective-permute-done.4.pb2), channel_id=1, source_target_pairs={{0,4},{4,8},{8,12},{1,5},{5,9},{9,13},{16,20},{20,24},{24,28},{17,... | collective-permute-start | bytes 786440 | tf_op jit(solution)/shard_map/ppermute | solution.py:610
  39.7 36.1 %collective-permute-start.1 = (bf16[512,256]{1,0:T(8,128)(2,1)}, bf16[512,256]{1,0:T(8,128)(2,1)S(1)}, u32[]{:S(2)}, u32[]{:S(2)}) collective-permute-start(bf16[512,256]{1,0:T(8,128)(2,1)} %copy-done.4), channel_id=1, source_target_pairs={{0,4},{4,8},{8,12},{1,5},{5,9},{9,13},{16,20},{20,24},{24,28},{17,... | collective-permute-start | bytes 786440 | tf_op jit(solution)/shard_map/ppermute | solution.py:610
  44.3 28.7 %collective-permute-start.10 = (bf16[512,512]{1,0:T(8,128)(2,1)S(1)}, bf16[512,512]{1,0:T(8,128)(2,1)S(1)}, u32[]{:S(2)}, u32[]{:S(2)}) collective-permute-start(bf16[512,512]{1,0:T(8,128)(2,1)S(1)} %broadcast_select_fusion.1), channel_id=1, source_target_pairs={{0,2},{2,0},{4,6},{6,4},{8,10},{10,8},{12,14},{14,12},{1,3},{3,1},... | collective-permute-start | bytes 1572872 | tf_op jit(solution)/shard_map/ppermute | solution.py:610
  44.5 23.1 %collective-permute-start.6 = (bf16[520,512]{1,0:T(8,128)(2,1)S(1)}, bf16[520,512]{1,0:T(8,128)(2,1)S(1)}, u32[]{:S(2)}, u32[]{:S(2)}) collective-permute-start(bf16[520,512]{1,0:T(8,128)(2,1)S(1)} %broadcast_select_fusion), channel_id=1, source_target_pairs={{0,2},{2,0},{4,6},{6,4},{8,10},{10,8},{12,14},{14,12},{1,3},{3,1},... | collective-permute-start | bytes 1597448 | tf_op jit(solution)/shard_map/ppermute | solution.py:610
  46.6 21.0 %collective-permute-start.3 = (bf16[520,512]{1,0:T(8,128)(2,1)}, bf16[520,512]{1,0:T(8,128)(2,1)S(1)}, u32[]{:S(2)}, u32[]{:S(2)}) collective-permute-start(bf16[520,512]{1,0:T(8,128)(2,1)} %collective-permute-done.2.pa.pb2.pb3), channel_id=1, source_target_pairs={{0,4},{4,8},{8,12},{1,5},{5,9},{9,13},{16,20},{20,24},{24,28},{17,... | collective-permute-start | bytes 1597448 | tf_op jit(solution)/shard_map/ppermute | solution.py:610
  50.1 1.6 %copy-start.13 = (f32[1024,512]{1,0:T(8,128)S(1)}, f32[1024,512]{1,0:T(8,128)}, u32[]{:S(2)}) copy-start(f32[1024,512]{1,0:T(8,128)} %copy-done.12) | copy-start | bytes 6291460
  51.7 1.6 %copy-start.15 = (f32[1024,512]{1,0:T(8,128)S(1)}, f32[1024,512]{1,0:T(8,128)}, u32[]{:S(2)}) copy-start(f32[1024,512]{1,0:T(8,128)} %copy-done.14) | copy-start | bytes 6291460
  53.3 1.6 %copy-start.17 = (f32[1024,512]{1,0:T(8,128)S(1)}, f32[1024,512]{1,0:T(8,128)}, u32[]{:S(2)}) copy-start(f32[1024,512]{1,0:T(8,128)} %copy-done.16) | copy-start | bytes 6291460
  54.9 4.0 %copy-start.7 = (f32[1024,512]{1,0:T(8,128)S(1)}, f32[1024,512]{1,0:T(8,128)}, u32[]{:S(2)}) copy-start(f32[1024,512]{1,0:T(8,128)} %copy-done.6) | copy-start | bytes 6291460
  54.9 4.0 %copy-start.9 = (f32[1024,512]{1,0:T(8,128)S(1)}, f32[1024,512]{1,0:T(8,128)}, u32[]{:S(2)}) copy-start(f32[1024,512]{1,0:T(8,128)} %copy-done.8) | copy-start | bytes 6291460
  54.9 4.0 %copy-start.11 = (f32[1024,512]{1,0:T(8,128)S(1)}, f32[1024,512]{1,0:T(8,128)}, u32[]{:S(2)}) copy-start(f32[1024,512]{1,0:T(8,128)} %copy-done.10) | copy-start | bytes 6291460

commit v2 on v1

--- a/solution.py
+++ b/solution.py
@@ -351,23 +351,35 @@
     hots = [one_hot_keys(seg[role, 0:1, :]) for role in range(2)]
     for role in range(2):
         fetch(role, zp.at[pair]).wait()
-    for role in range(2):
-        base = role * HALF
-        for g in range(PAIR):
-            q2 = stacked_queries(q, hot, base, (PAIR * h + g) * GROUPS)
-            keys = far[role, :, head_cols(g)]
-            k_aug = jnp.concatenate([keys, hots[role]], axis=1)
-            scores = triangle_scores(q2, k_aug, True)
-            old = load_state(mx0, base, g)
-            tops = [jnp.maximum(m, row_max(parts)) for m, parts in zip(old, scores)]
-            probs = [weights(parts, m) for parts, m in zip(scores, tops)]
-            v_aug = with_ones(far[role, :, head_cols(PAIR + g)])
-            o = triangle_values(probs, v_aug, True)
-            for i, mine, rows, cols in state_slices(base, g):
-                keep = jnp.exp2((old[i][mine] - tops[i][mine]) * EXP_SCALE)
-                acc[rows, cols] = keep * acc0[rows, cols] + o[i][mine, :HEAD_DIM]
-                ls[rows, cols] = keep * ls0[rows, cols] + o[i][mine, HEAD_DIM:]
-                mx[rows, cols] = tops[i][mine]
+
+    def go(roles):
+        for role in roles:
+            base = role * HALF
+            for g in range(PAIR):
+                q2 = stacked_queries(q, hot, base, (PAIR * h + g) * GROUPS)
+                keys = far[role, :, head_cols(g)]
+                k_aug = jnp.concatenate([keys, hots[role]], axis=1)
+                scores = triangle_scores(q2, k_aug, True)
+                old = load_state(mx0, base, g)
+                tops = [jnp.maximum(m, row_max(parts)) for m, parts in zip(old, scores)]
+                probs = [weights(parts, m) for parts, m in zip(scores, tops)]
+                v_aug = with_ones(far[role, :, head_cols(PAIR + g)])
+                o = triangle_values(probs, v_aug, True)
+                for i, mine, rows, cols in state_slices(base, g):
+                    keep = jnp.exp2((old[i][mine] - tops[i][mine]) * EXP_SCALE)
+                    acc[rows, cols] = keep * acc0[rows, cols] + o[i][mine, :HEAD_DIM]
+                    ls[rows, cols] = keep * ls0[rows, cols] + o[i][mine, HEAD_DIM:]
+                    mx[rows, cols] = tops[i][mine]
+
+    @pl.when(idx[0] > 0)
+    def _():
+        go((0, 1))
+
+    @pl.when(idx[0] == 0)
+    def _():
+        go((1,))
+        for old, new in ((acc0, acc), (mx0, mx), (ls0, ls)):
+            new[0:HALF, :] = old[0:HALF, :]
 
 
 def far(h, n, idx, q, hot, zp, za, zb, pa, pb2, pb3, state):

time: 76.7 us -> 76.8 us (level)
  Pallas kernels: 25.3 us -> 23.4 us
  waiting for transfers between devices: 8.73 us -> 10.5 us
    pallas_call x2, Pallas kernels: 7.69 us -> 5.78 us  [far(): pl.pallas_call(functools.partial(far_kernel, h, n), out_shape=(STATE,) *...]
    ppermute x11, waiting for transfers between devices: 8.73 us -> 10.5 us  [send(): return lax.ppermute(x, 'seq', route)]
  transfers between devices with their start and end apart: 11 -> 11, of which waited for: 2 -> 2; matrix products, arithmetic and copies ran while one was open for 2% -> 2% of each run, Pallas kernels for 30% -> 28%
where the time goes in v2:
time: 76.8 us; the launch traced here: 76.1 us
  starting transfers between devices  27.2 us (35%)
  Pallas kernels  23.4 us (30%)
  local copies, waits for them, and re-layouts  13.1 us (17%)
  waiting for transfers between devices  10.5 us (14%)
  other arithmetic  1.38 us (2%)
    ppermute x11, starting transfers between devices, send(): return lax.ppermute(x, 'seq', route)  27.2 us
    unnamed x38, local copies, waits for them, and re-layouts  13.1 us
    ppermute x11, waiting for transfers between devices, send(): return lax.ppermute(x, 'seq', route)  10.5 us
    pallas_call x2, Pallas kernels, far(): pl.pallas_call(functools.partial(far_kernel, h, n), out_shape=(STATE,) *...  5.78 us
    pallas_call x1, Pallas kernels, first_pair(): pl.pallas_call(functools.partial(first_pair_kernel, n), out_shape=(jax.Sh...  5.27 us
    pallas_call x2, Pallas kernels, own(): pl.pallas_call(functools.partial(own_kernel, h), out_shape=(STATE,) * 3,...  4.6 us
    pallas_call x2, Pallas kernels, second_pair(): pl.pallas_call(functools.partial(second_pair_kernel, n), out_shape=jax.Sh...  2.96 us
    pallas_call x1, Pallas kernels, pack_rest(): pl.pallas_call(pack_rest_kernel, out_shape=tuple((jax.ShapeDtypeStruct(x,...  2.43 us
  transfers between devices with their start and end apart: 11, of which 2 were waited for; matrix products, arithmetic and copies ran while one was open for 2% of the time, Pallas kernels for 28%

profile of v2, /device:TPU:0, one launch (start us, length us, event | category | flops | bytes accessed | tf_op | source)
XLA Modules:
  0.0 76.1 jit_solution(5579733073458172142)
XLA Ops:
  0.0 2.4 %pack1.1 = (bf16[520,512]{1,0:T(8,128)(2,1)S(1)}, bf16[512,256]{1,0:T(8,128)(2,1)}, bf16[512,256]{1,0:T(8,128)(2,1)S(1)}, bf16[512,512]{1,0:T(8,128)(2,1)}) custom-call(bf16[1024,512]{1,0:T(8,128)(2,1)} %k.9, bf16[1024,512]{1,0:T(8,128)(2,1)} %v.9, s32[1,1024]{1,0:T(1,128)} %bitcast.2), custom_call_target="tpu_custom_call" | custom-call | flops 1048576 | bytes 3145728 | tf_op jit(solution)/shard_map/pack1/pallas_call | solution.py:165
  2.5 1.3 %collective-permute-start.5 = (bf16[520,512]{1,0:T(8,128)(2,1)S(1)}, bf16[520,512]{1,0:T(8,128)(2,1)S(1)}, u32[]{:S(2)}, u32[]{:S(2)}) collective-permute-start(bf16[520,512]{1,0:T(8,128)(2,1)S(1)} %get-tuple-element.28), channel_id=1, source_target_pairs={{4,0},{6,2},{8,4},{10,6},{12,8},{14,10},{5,1},{7,3},{9,5},{11,7},{... | collective-permute-start | bytes 1597448 | tf_op jit(solution)/shard_map/ppermute | solution.py:622
  3.8 2.4 %pack0.1 = (bf16[520,512]{1,0:T(8,128)(2,1)}, bf16[1040,512]{1,0:T(8,128)(2,1)}) custom-call(bf16[1024,512]{1,0:T(8,128)(2,1)} %k.9, bf16[1024,512]{1,0:T(8,128)(2,1)} %v.9, s32[1,1024]{1,0:T(1,128)} %bitcast.3), custom_call_target="tpu_custom_call" | custom-call | flops 1048576 | bytes 2097152 | tf_op jit(solution)/shard_map/pack0/pallas_call | solution.py:94
  6.1 3.1 %collective-permute-start.2 = (bf16[520,512]{1,0:T(8,128)(2,1)}, bf16[520,512]{1,0:T(8,128)(2,1)}, u32[]{:S(2)}, u32[]{:S(2)}) collective-permute-start(bf16[520,512]{1,0:T(8,128)(2,1)} %get-tuple-element.26.f1), channel_id=1, source_target_pairs={{0,2},{2,0},{4,6},{6,4},{8,10},{10,8},{12,14},{14,12},{1,3},{3,1},... | collective-permute-start | bytes 1597448 | tf_op jit(solution)/shard_map/ppermute | solution.py:622
  9.2 1.3 %collective-permute-start.8 = (bf16[512,512]{1,0:T(8,128)(2,1)}, bf16[512,512]{1,0:T(8,128)(2,1)}, u32[]{:S(2)}, u32[]{:S(2)}) collective-permute-start(bf16[512,512]{1,0:T(8,128)(2,1)} %get-tuple-element.36), channel_id=1, source_target_pairs={{4,0},{6,2},{8,4},{10,6},{12,8},{14,10},{5,1},{7,3},{9,5},{11,7},{... | collective-permute-start | bytes 1572872 | tf_op jit(solution)/shard_map/ppermute | solution.py:622
  10.5 0.1 collective-permute-start
  10.6 6.2 %collective-permute-start.7 = (bf16[1040,512]{1,0:T(8,128)(2,1)}, bf16[1040,512]{1,0:T(8,128)(2,1)}, u32[]{:S(2)}, u32[]{:S(2)}) collective-permute-start(bf16[1040,512]{1,0:T(8,128)(2,1)} %get-tuple-element.29), channel_id=1, source_target_pairs={{0,4},{2,6},{4,8},{6,10},{8,12},{10,14},{1,5},{3,7},{5,9},{7,11},{... | collective-permute-start | bytes 3194888 | tf_op jit(solution)/shard_map/ppermute | solution.py:622
  16.8 0.2 fusion.hot
  17.0 2.3 %shard_map.48 = (f32[1024,512]{1,0:T(8,128)S(1)}, f32[1024,512]{1,0:T(8,128)S(1)}, f32[1024,512]{1,0:T(8,128)S(1)}) custom-call(bf16[1024,1024]{1,0:T(8,128)(2,1)S(1)} %copy-done.2, bf16[1024,512]{1,0:T(8,128)(2,1)S(1)} %copy-done, bf16[1024,512]{1,0:T(8,128)(2,1)S(1)} %copy-done.1, bf16[1024,128]{1,0:T(8,128)(2,1)S(1)} %fusion.hot), custom_call_target="tpu_custom_call" | custom-call | flops 5368709120 | bytes 8388608 | tf_op jit(solution)/shard_map/pallas_call | solution.py:300
  19.3 1.3 %copy-done.12 = f32[1024,512]{1,0:T(8,128)} copy-done((f32[1024,512]{1,0:T(8,128)}, f32[1024,512]{1,0:T(8,128)S(1)}, u32[]{:S(2)}) %copy-start.12) | copy-done | bytes 2097176
  20.7 1.3 %copy-done.14 = f32[1024,512]{1,0:T(8,128)} copy-done((f32[1024,512]{1,0:T(8,128)}, f32[1024,512]{1,0:T(8,128)S(1)}, u32[]{:S(2)}) %copy-start.14) | copy-done | bytes 2097176
  22.0 1.4 %copy-done.16 = f32[1024,512]{1,0:T(8,128)} copy-done((f32[1024,512]{1,0:T(8,128)}, f32[1024,512]{1,0:T(8,128)S(1)}, u32[]{:S(2)}) %copy-start.16) | copy-done | bytes 2097176
  23.4 3.7 %collective-permute-done.pb3 = bf16[512,256]{1,0:T(8,128)(2,1)S(1)} collective-permute-done((bf16[512,256]{1,0:T(8,128)(2,1)S(1)}, bf16[512,256]{1,0:T(8,128)(2,1)S(1)}, u32[]{:S(2)}, u32[]{:S(2)}) %collective-permute-start) | collective-permute-done | bytes 262176 | tf_op jit(solution)/shard_map/ppermute | solution.py:622
  27.1 1.7 %collective-permute-start.4 = (bf16[512,256]{1,0:T(8,128)(2,1)}, bf16[512,256]{1,0:T(8,128)(2,1)}, u32[]{:S(2)}, u32[]{:S(2)}) collective-permute-start(bf16[512,256]{1,0:T(8,128)(2,1)} %get-tuple-element.27), channel_id=1, source_target_pairs={{0,2},{2,0},{4,6},{6,4},{8,10},{10,8},{12,14},{14,12},{1,3},{3,1},... | collective-permute-start | bytes 786440 | tf_op jit(solution)/shard_map/ppermute | solution.py:622
  28.9 2.3 %shard_map.46 = (f32[1024,512]{1,0:T(8,128)S(1)}, f32[1024,512]{1,0:T(8,128)S(1)}, f32[1024,512]{1,0:T(8,128)S(1)}) custom-call(bf16[1024,1024]{1,0:T(8,128)(2,1)S(1)} %copy-done.2, bf16[1024,512]{1,0:T(8,128)(2,1)S(1)} %copy-done, bf16[1024,512]{1,0:T(8,128)(2,1)S(1)} %copy-done.1, bf16[1024,128]{1,0:T(8,128)(2,1)S(1)} %fusion.hot), custom_call_target="tpu_custom_call" | custom-call | flops 5368709120 | bytes 8388608 | tf_op jit(solution)/shard_map/pallas_call | solution.py:300
  31.2 1.3 %copy-done.6 = f32[1024,512]{1,0:T(8,128)} copy-done((f32[1024,512]{1,0:T(8,128)}, f32[1024,512]{1,0:T(8,128)S(1)}, u32[]{:S(2)}) %copy-start.6) | copy-done | bytes 2097176
  32.5 1.4 %copy-done.8 = f32[1024,512]{1,0:T(8,128)} copy-done((f32[1024,512]{1,0:T(8,128)}, f32[1024,512]{1,0:T(8,128)S(1)}, u32[]{:S(2)}) %copy-start.8) | copy-done | bytes 2097176
  33.9 1.4 %copy-done.10 = f32[1024,512]{1,0:T(8,128)} copy-done((f32[1024,512]{1,0:T(8,128)}, f32[1024,512]{1,0:T(8,128)S(1)}, u32[]{:S(2)}) %copy-start.10) | copy-done | bytes 2097176
  35.3 4.4 %collective-permute-start.9 = (bf16[512,256]{1,0:T(8,128)(2,1)}, bf16[512,256]{1,0:T(8,128)(2,1)S(1)}, u32[]{:S(2)}, u32[]{:S(2)}) collective-permute-start(bf16[512,256]{1,0:T(8,128)(2,1)} %collective-permute-done.4.pb2), channel_id=1, source_target_pairs={{0,4},{4,8},{8,12},{1,5},{5,9},{9,13},{16,20},{20,24},{24,28},{17,... | collective-permute-start | bytes 786440 | tf_op jit(solution)/shard_map/ppermute | solution.py:622
  39.7 3.5 %collective-permute-start.1 = (bf16[512,256]{1,0:T(8,128)(2,1)}, bf16[512,256]{1,0:T(8,128)(2,1)S(1)}, u32[]{:S(2)}, u32[]{:S(2)}) collective-permute-start(bf16[512,256]{1,0:T(8,128)(2,1)} %copy-done.4), channel_id=1, source_target_pairs={{0,4},{4,8},{8,12},{1,5},{5,9},{9,13},{16,20},{20,24},{24,28},{17,... | collective-permute-start | bytes 786440 | tf_op jit(solution)/shard_map/ppermute | solution.py:622
  43.2 1.1 %broadcast_select_fusion.1 = bf16[512,512]{1,0:T(8,128)(2,1)S(1)} fusion(bf16[512,512]{1,0:T(8,128)(2,1)} %collective-permute-done.8.zb, bf16[512,512]{1,0:T(8,128)(2,1)} %get-tuple-element.36, pred[]{:T(512)S(6)} %eq.21), kind=kLoop, calls=%fused_computation.3 | loop fusion | flops 262144 | bytes 1572865 | tf_op jit(solution)/shard_map/jit(_where)/select_n | solution.py:645
  44.5 2.1 %collective-permute-start.6 = (bf16[520,512]{1,0:T(8,128)(2,1)S(1)}, bf16[520,512]{1,0:T(8,128)(2,1)S(1)}, u32[]{:S(2)}, u32[]{:S(2)}) collective-permute-start(bf16[520,512]{1,0:T(8,128)(2,1)S(1)} %broadcast_select_fusion), channel_id=1, source_target_pairs={{0,2},{2,0},{4,6},{6,4},{8,10},{10,8},{12,14},{14,12},{1,3},{3,1},... | collective-permute-start | bytes 1597448 | tf_op jit(solution)/shard_map/ppermute | solution.py:622
  46.6 3.5 %collective-permute-start.3 = (bf16[520,512]{1,0:T(8,128)(2,1)}, bf16[520,512]{1,0:T(8,128)(2,1)S(1)}, u32[]{:S(2)}, u32[]{:S(2)}) collective-permute-start(bf16[520,512]{1,0:T(8,128)(2,1)} %collective-permute-done.2.pa.pb2.pb3), channel_id=1, source_target_pairs={{0,4},{4,8},{8,12},{1,5},{5,9},{9,13},{16,20},{20,24},{24,28},{17,... | collective-permute-start | bytes 1597448 | tf_op jit(solution)/shard_map/ppermute | solution.py:622
  50.1 1.6 %copy-done.13 = f32[1024,512]{1,0:T(8,128)S(1)} copy-done((f32[1024,512]{1,0:T(8,128)S(1)}, f32[1024,512]{1,0:T(8,128)}, u32[]{:S(2)}) %copy-start.13) | copy-done | bytes 2097176
  51.7 1.6 %copy-done.15 = f32[1024,512]{1,0:T(8,128)S(1)} copy-done((f32[1024,512]{1,0:T(8,128)S(1)}, f32[1024,512]{1,0:T(8,128)}, u32[]{:S(2)}) %copy-start.15) | copy-done | bytes 2097176
  53.3 1.6 %copy-done.17 = f32[1024,512]{1,0:T(8,128)S(1)} copy-done((f32[1024,512]{1,0:T(8,128)S(1)}, f32[1024,512]{1,0:T(8,128)}, u32[]{:S(2)}) %copy-start.17) | copy-done | bytes 2097176
  54.9 3.0 %shard_map.49 = (f32[1024,512]{1,0:T(8,128)S(1)}, f32[1024,512]{1,0:T(8,128)S(1)}, f32[1024,512]{1,0:T(8,128)S(1)}) custom-call(s32[1]{0:T(128)} %bitcast.idx, bf16[1024,1024]{1,0:T(8,128)(2,1)S(1)} %copy-done.3, bf16[1024,128]{1,0:T(8,128)(2,1)S(1)} %fusion.hot, bf16[1040,512]{1,0:T(8,128)(2,1)} %collective-permute-done.7.zp, ...), custom_call_target="tpu_custom_call" | custom-call | flops 5368709120 | bytes 8388608 | tf_op jit(solution)/shard_map/pallas_call | solution.py:386
  58.0 0.1 copy-done.11
  58.1 2.7 %shard_map.47 = (f32[1024,512]{1,0:T(8,128)S(1)}, f32[1024,512]{1,0:T(8,128)S(1)}, f32[1024,512]{1,0:T(8,128)S(1)}) custom-call(s32[1]{0:T(128)} %bitcast.idx, bf16[1024,1024]{1,0:T(8,128)(2,1)S(1)} %copy-done.3, bf16[1024,128]{1,0:T(8,128)(2,1)S(1)} %fusion.hot, bf16[1040,512]{1,0:T(8,128)(2,1)} %collective-permute-done.7.zp, ...), custom_call_target="tpu_custom_call" | custom-call | flops 5368709120 | bytes 8388608 | tf_op jit(solution)/shard_map/pallas_call | solution.py:386
  60.8 6.8 %collective-permute-done.6.d1 = bf16[520,512]{1,0:T(8,128)(2,1)S(1)} collective-permute-done((bf16[520,512]{1,0:T(8,128)(2,1)S(1)}, bf16[520,512]{1,0:T(8,128)(2,1)S(1)}, u32[]{:S(2)}, u32[]{:S(2)}) %collective-permute-start.6) | collective-permute-done | bytes 532512 | tf_op jit(solution)/shard_map/ppermute | solution.py:622
  67.6 5.3 %last0.1 = (bf16[1024,1024]{1,0:T(8,128)(2,1)}, bf16[2,512,128]{2,1,0:T(8,128)(2,1)S(1)}) custom-call(s32[1]{0:T(128)} %bitcast.idx, bf16[1024,1024]{1,0:T(8,128)(2,1)S(1)} %copy-done.3, bf16[1024,128]{1,0:T(8,128)(2,1)S(1)} %fusion.hot, bf16[520,512]{1,0:T(8,128)(2,1)S(1)} %collective-permute-done.3.r1, bf16[520,512]{1,0:T(8,128)(2,1)} %collective-permute-done.2.pa.pb2.pb3, ...), custom_call_target="tpu_custom_call" | custom-call | flops 5368709120 | bytes 8388608 | tf_op jit(solution)/shard_map/last0/pallas_call | solution.py:539
  72.9 2.9 %shard_map.50.rest_5_ = bf16[1024,1024]{1,0:T(8,128)(2,1)} custom-call(s32[1]{0:T(128)} %bitcast.idx, bf16[1024,1024]{1,0:T(8,128)(2,1)S(1)} %copy-done.3, bf16[1024,128]{1,0:T(8,128)(2,1)S(1)} %fusion.hot, bf16[512,256]{1,0:T(8,128)(2,1)S(1)} %collective-permute-done.9.rest_0_, ...), custom_call_target="tpu_custom_call", output_to_operand_aliasing={{}: (9, {})} | custom-call | flops 5368709120 | bytes 8388608 | tf_op jit(solution)/shard_map/pallas_call | solution.py:597
  (41 shorter events, 0.3 us)
Async XLA Ops:
  0.0 16.8 %copy-start.18 = (s32[1024]{0:T(1024)S(1)}, s32[1024]{0:T(1024)}, u32[]{:S(2)}) copy-start(s32[1024]{0:T(1024)} %param.7) | copy-start | bytes 12292
  0.0 17.0 %copy-start = (bf16[1024,512]{1,0:T(8,128)(2,1)S(1)}, bf16[1024,512]{1,0:T(8,128)(2,1)}, u32[]{:S(2)}) copy-start(bf16[1024,512]{1,0:T(8,128)(2,1)} %k.9) | copy-start | bytes 3145732
  0.0 17.0 %copy-start.1 = (bf16[1024,512]{1,0:T(8,128)(2,1)S(1)}, bf16[1024,512]{1,0:T(8,128)(2,1)}, u32[]{:S(2)}) copy-start(bf16[1024,512]{1,0:T(8,128)(2,1)} %v.9) | copy-start | bytes 3145732
  0.0 17.0 %copy-start.2 = (bf16[1024,1024]{1,0:T(8,128)(2,1)S(1)}, bf16[1024,1024]{1,0:T(8,128)(2,1)}, u32[]{:S(2)}) copy-start(bf16[1024,1024]{1,0:T(8,128)(2,1)} %q.13) | copy-start | bytes 6291460
  2.5 41.9 %collective-permute-start.5 = (bf16[520,512]{1,0:T(8,128)(2,1)S(1)}, bf16[520,512]{1,0:T(8,128)(2,1)S(1)}, u32[]{:S(2)}, u32[]{:S(2)}) collective-permute-start(bf16[520,512]{1,0:T(8,128)(2,1)S(1)} %get-tuple-element.28), channel_id=1, source_target_pairs={{4,0},{6,2},{8,4},{10,6},{12,8},{14,10},{5,1},{7,3},{9,5},{11,7},{... | collective-permute-start | bytes 1597448 | tf_op jit(solution)/shard_map/ppermute | solution.py:622
  6.1 38.4 %collective-permute-start.2 = (bf16[520,512]{1,0:T(8,128)(2,1)}, bf16[520,512]{1,0:T(8,128)(2,1)}, u32[]{:S(2)}, u32[]{:S(2)}) collective-permute-start(bf16[520,512]{1,0:T(8,128)(2,1)} %get-tuple-element.26.f1), channel_id=1, source_target_pairs={{0,2},{2,0},{4,6},{6,4},{8,10},{10,8},{12,14},{14,12},{1,3},{3,1},... | collective-permute-start | bytes 1597448 | tf_op jit(solution)/shard_map/ppermute | solution.py:622
  9.2 30.5 %collective-permute-start.8 = (bf16[512,512]{1,0:T(8,128)(2,1)}, bf16[512,512]{1,0:T(8,128)(2,1)}, u32[]{:S(2)}, u32[]{:S(2)}) collective-permute-start(bf16[512,512]{1,0:T(8,128)(2,1)} %get-tuple-element.36), channel_id=1, source_target_pairs={{4,0},{6,2},{8,4},{10,6},{12,8},{14,10},{5,1},{7,3},{9,5},{11,7},{... | collective-permute-start | bytes 1572872 | tf_op jit(solution)/shard_map/ppermute | solution.py:622
  10.5 16.6 %collective-permute-start = (bf16[512,256]{1,0:T(8,128)(2,1)S(1)}, bf16[512,256]{1,0:T(8,128)(2,1)S(1)}, u32[]{:S(2)}, u32[]{:S(2)}) collective-permute-start(bf16[512,256]{1,0:T(8,128)(2,1)S(1)} %get-tuple-element.25), channel_id=1, source_target_pairs={{0,2},{2,0},{4,6},{6,4},{8,10},{10,8},{12,14},{14,12},{1,3},{3,1},... | collective-permute-start | bytes 786440 | tf_op jit(solution)/shard_map/ppermute | solution.py:622
  10.6 36.0 %collective-permute-start.7 = (bf16[1040,512]{1,0:T(8,128)(2,1)}, bf16[1040,512]{1,0:T(8,128)(2,1)}, u32[]{:S(2)}, u32[]{:S(2)}) collective-permute-start(bf16[1040,512]{1,0:T(8,128)(2,1)} %get-tuple-element.29), channel_id=1, source_target_pairs={{0,4},{2,6},{4,8},{6,10},{8,12},{10,14},{1,5},{3,7},{5,9},{7,11},{... | collective-permute-start | bytes 3194888 | tf_op jit(solution)/shard_map/ppermute | solution.py:622
  19.3 1.3 %copy-start.12 = (f32[1024,512]{1,0:T(8,128)}, f32[1024,512]{1,0:T(8,128)S(1)}, u32[]{:S(2)}) copy-start(f32[1024,512]{1,0:T(8,128)S(1)} %get-tuple-element.37.rest_0_) | copy-start | bytes 6291460
  20.7 1.3 %copy-start.14 = (f32[1024,512]{1,0:T(8,128)}, f32[1024,512]{1,0:T(8,128)S(1)}, u32[]{:S(2)}) copy-start(f32[1024,512]{1,0:T(8,128)S(1)} %get-tuple-element.38.rest_1_) | copy-start | bytes 6291460
  22.0 1.4 %copy-start.16 = (f32[1024,512]{1,0:T(8,128)}, f32[1024,512]{1,0:T(8,128)S(1)}, u32[]{:S(2)}) copy-start(f32[1024,512]{1,0:T(8,128)S(1)} %get-tuple-element.39.rest_2_) | copy-start | bytes 6291460
  27.1 4.0 %copy-start.4 = (bf16[512,256]{1,0:T(8,128)(2,1)}, bf16[512,256]{1,0:T(8,128)(2,1)S(1)}, u32[]{:S(2)}) copy-start(bf16[512,256]{1,0:T(8,128)(2,1)S(1)} %collective-permute-done.pb3) | copy-start | bytes 786436
  27.1 8.2 %collective-permute-start.4 = (bf16[512,256]{1,0:T(8,128)(2,1)}, bf16[512,256]{1,0:T(8,128)(2,1)}, u32[]{:S(2)}, u32[]{:S(2)}) collective-permute-start(bf16[512,256]{1,0:T(8,128)(2,1)} %get-tuple-element.27), channel_id=1, source_target_pairs={{0,2},{2,0},{4,6},{6,4},{8,10},{10,8},{12,14},{14,12},{1,3},{3,1},... | collective-permute-start | bytes 786440 | tf_op jit(solution)/shard_map/ppermute | solution.py:622
  31.2 1.3 %copy-start.6 = (f32[1024,512]{1,0:T(8,128)}, f32[1024,512]{1,0:T(8,128)S(1)}, u32[]{:S(2)}) copy-start(f32[1024,512]{1,0:T(8,128)S(1)} %get-tuple-element.30.rest_0_) | copy-start | bytes 6291460
  32.5 1.4 %copy-start.8 = (f32[1024,512]{1,0:T(8,128)}, f32[1024,512]{1,0:T(8,128)S(1)}, u32[]{:S(2)}) copy-start(f32[1024,512]{1,0:T(8,128)S(1)} %get-tuple-element.31.rest_1_) | copy-start | bytes 6291460
  33.9 1.4 %copy-start.10 = (f32[1024,512]{1,0:T(8,128)}, f32[1024,512]{1,0:T(8,128)S(1)}, u32[]{:S(2)}) copy-start(f32[1024,512]{1,0:T(8,128)S(1)} %get-tuple-element.32.rest_2_) | copy-start | bytes 6291460
  35.3 14.8 %copy-start.3 = (bf16[1024,1024]{1,0:T(8,128)(2,1)S(1)}, bf16[1024,1024]{1,0:T(8,128)(2,1)}, u32[]{:S(2)}) copy-start(bf16[1024,1024]{1,0:T(8,128)(2,1)} %q.13) | copy-start | bytes 6291460
  35.3 14.8 %copy-start.5 = (bf16[512,256]{1,0:T(8,128)(2,1)S(1)}, bf16[512,256]{1,0:T(8,128)(2,1)}, u32[]{:S(2)}) copy-start(bf16[512,256]{1,0:T(8,128)(2,1)} %copy-done.4) | copy-start | bytes 786436
  35.3 37.6 %collective-permute-start.9 = (bf16[512,256]{1,0:T(8,128)(2,1)}, bf16[512,256]{1,0:T(8,128)(2,1)S(1)}, u32[]{:S(2)}, u32[]{:S(2)}) collective-permute-start(bf16[512,256]{1,0:T(8,128)(2,1)} %collective-permute-done.4.pb2), channel_id=1, source_target_pairs={{0,4},{4,8},{8,12},{1,5},{5,9},{9,13},{16,20},{20,24},{24,28},{17,... | collective-permute-start | bytes 786440 | tf_op jit(solution)/shard_map/ppermute | solution.py:622
  39.7 36.1 %collective-permute-start.1 = (bf16[512,256]{1,0:T(8,128)(2,1)}, bf16[512,256]{1,0:T(8,128)(2,1)S(1)}, u32[]{:S(2)}, u32[]{:S(2)}) collective-permute-start(bf16[512,256]{1,0:T(8,128)(2,1)} %copy-done.4), channel_id=1, source_target_pairs={{0,4},{4,8},{8,12},{1,5},{5,9},{9,13},{16,20},{20,24},{24,28},{17,... | collective-permute-start | bytes 786440 | tf_op jit(solution)/shard_map/ppermute | solution.py:622
  44.3 28.6 %collective-permute-start.10 = (bf16[512,512]{1,0:T(8,128)(2,1)S(1)}, bf16[512,512]{1,0:T(8,128)(2,1)S(1)}, u32[]{:S(2)}, u32[]{:S(2)}) collective-permute-start(bf16[512,512]{1,0:T(8,128)(2,1)S(1)} %broadcast_select_fusion.1), channel_id=1, source_target_pairs={{0,2},{2,0},{4,6},{6,4},{8,10},{10,8},{12,14},{14,12},{1,3},{3,1},... | collective-permute-start | bytes 1572872 | tf_op jit(solution)/shard_map/ppermute | solution.py:622
  44.5 23.1 %collective-permute-start.6 = (bf16[520,512]{1,0:T(8,128)(2,1)S(1)}, bf16[520,512]{1,0:T(8,128)(2,1)S(1)}, u32[]{:S(2)}, u32[]{:S(2)}) collective-permute-start(bf16[520,512]{1,0:T(8,128)(2,1)S(1)} %broadcast_select_fusion), channel_id=1, source_target_pairs={{0,2},{2,0},{4,6},{6,4},{8,10},{10,8},{12,14},{14,12},{1,3},{3,1},... | collective-permute-start | bytes 1597448 | tf_op jit(solution)/shard_map/ppermute | solution.py:622
  46.6 21.0 %collective-permute-start.3 = (bf16[520,512]{1,0:T(8,128)(2,1)}, bf16[520,512]{1,0:T(8,128)(2,1)S(1)}, u32[]{:S(2)}, u32[]{:S(2)}) collective-permute-start(bf16[520,512]{1,0:T(8,128)(2,1)} %collective-permute-done.2.pa.pb2.pb3), channel_id=1, source_target_pairs={{0,4},{4,8},{8,12},{1,5},{5,9},{9,13},{16,20},{20,24},{24,28},{17,... | collective-permute-start | bytes 1597448 | tf_op jit(solution)/shard_map/ppermute | solution.py:622
  50.1 1.6 %copy-start.13 = (f32[1024,512]{1,0:T(8,128)S(1)}, f32[1024,512]{1,0:T(8,128)}, u32[]{:S(2)}) copy-start(f32[1024,512]{1,0:T(8,128)} %copy-done.12) | copy-start | bytes 6291460
  51.7 1.6 %copy-start.15 = (f32[1024,512]{1,0:T(8,128)S(1)}, f32[1024,512]{1,0:T(8,128)}, u32[]{:S(2)}) copy-start(f32[1024,512]{1,0:T(8,128)} %copy-done.14) | copy-start | bytes 6291460
  53.3 1.6 %copy-start.17 = (f32[1024,512]{1,0:T(8,128)S(1)}, f32[1024,512]{1,0:T(8,128)}, u32[]{:S(2)}) copy-start(f32[1024,512]{1,0:T(8,128)} %copy-done.16) | copy-start | bytes 6291460
  54.9 3.1 %copy-start.7 = (f32[1024,512]{1,0:T(8,128)S(1)}, f32[1024,512]{1,0:T(8,128)}, u32[]{:S(2)}) copy-start(f32[1024,512]{1,0:T(8,128)} %copy-done.6) | copy-start | bytes 6291460
  54.9 3.1 %copy-start.9 = (f32[1024,512]{1,0:T(8,128)S(1)}, f32[1024,512]{1,0:T(8,128)}, u32[]{:S(2)}) copy-start(f32[1024,512]{1,0:T(8,128)} %copy-done.8) | copy-start | bytes 6291460
  54.9 3.2 %copy-start.11 = (f32[1024,512]{1,0:T(8,128)S(1)}, f32[1024,512]{1,0:T(8,128)}, u32[]{:S(2)}) copy-start(f32[1024,512]{1,0:T(8,128)} %copy-done.10) | copy-start | bytes 6291460
